TPU v7x, 256 devices: a whole 4x4x8 slice. The times are simulated.
256 devices in a mesh: grp: 4 (over z_hi), tile: 64 (over x, z_lo, y, core).
Axes of the slice: x: 4, y: 4, z: 8 (z_hi: 4, z_lo: 2; z = z_hi * 2 + z_lo), core: 2. Of those that a mesh axis runs over, the one named last changes fastest.
Arguments:
- ocean_state: bfloat16 [64, 4096, 512], P(None, 'tile', 'grp'), may hold values from -8 to 8
- sea_mask: int32 [4096, 512], P('tile', 'grp'), may hold values 0 or 1
- spectral_weights: float32 [2, 2, 32, 64, 64], replicated, may hold values from -0.75 to 0.75
- point_weights: bfloat16 [2, 64, 64], replicated, may hold values from -0.75 to 0.75
- point_bias: float32 [2, 64], replicated, may hold values from -4 to 4
- inner_weights: bfloat16 [2, 128, 64], replicated, may hold values from -0.75 to 0.75
- outer_weights: bfloat16 [2, 64, 128], replicated, may hold values from -0.5 to 0.5
- coarse_spectral: float32 [2, 32, 64, 64], replicated, may hold values from -0.75 to 0.75
- coarse_point: float32 [64, 64], replicated, may hold values from -0.75 to 0.75
- coarse_bias: float32 [64], replicated, may hold values from -2.5 to 2.5
Outputs:
- corrected: bfloat16 [64, 4096, 512], P(None, 'tile', 'grp')
Inputs may be any that keep to these rules, and one draw needn't show every extreme that they name: `sea_mask`: 1 marks a sea cell, 0 a land cell.
All inputs are finite; a program needn't handle non-finite values. No bound on the sum of `sea_mask` on one device may be relied on, other than what follows from the above.
Results may differ from a plain program's by a relative error of at most 0.0065.
Values may be sent and summed in bfloat16 or wider, within the bound.
A program may use at most 64 MiB of HBM per device.

v0:
```python
import math

import jax
import jax.numpy as jnp
from jax import lax
from jax.sharding import PartitionSpec as P

H = 64
R = 16
MX = 8
MY = 4
LAYERS = 2


PRECISE = lax.Precision.HIGHEST


def with_halo(x, sides, width):
    for axis, dim in sides:
        devices, length = (lax.axis_size(axis), x.shape[dim])
        up = [(i, (i + 1) % devices) for i in range(devices - 1)]
        down = [(j, i) for i, j in up]
        last = lax.slice_in_dim(x, length - width, length, axis=dim)
        first = lax.slice_in_dim(x, 0, width, axis=dim)
        before = lax.ppermute(last, axis, up)
        after = lax.ppermute(first, axis, down)
        x = jnp.concatenate([before, x, after], axis=dim)
    return x


def wave_numbers():
    order = jnp.arange(MX, dtype=jnp.int32)
    return jnp.where(order < MX // 2, order, order - MX)


def masked_table(positions, numbers, length):
    cycles = positions[:, None] * numbers[None, :] % length
    radians = cycles.astype(jnp.float32) * (2.0 * math.pi / length)
    inside = ((positions >= 0) & (positions < length)).astype(jnp.float32)[:, None]
    return (jnp.cos(radians) * inside, jnp.sin(radians) * inside)


def columns_transform(values, col_positions, col_length):
    channels, row_count, col_count = values.shape
    cos_cols, sin_cols = masked_table(col_positions, jnp.arange(MY, dtype=jnp.int32), col_length)
    lookup = jnp.concatenate([cos_cols, -sin_cols], axis=1)
    flattened = values.reshape(channels * row_count, col_count)
    return jnp.dot(
        flattened, lookup, precision=PRECISE, preferred_element_type=jnp.float32
    ).reshape(channels, row_count, 2 * MY)


def rows_transform(y_modes, row_positions, row_length):
    cos_rows, sin_rows = masked_table(row_positions, wave_numbers(), row_length)
    real_in = y_modes[:, :, :MY]
    imag_in = y_modes[:, :, MY:]
    coef_real = jnp.einsum("cxj,xi->cij", real_in, cos_rows, precision=PRECISE) + jnp.einsum(
        "cxj,xi->cij", imag_in, sin_rows, precision=PRECISE
    )
    coef_imag = jnp.einsum("cxj,xi->cij", imag_in, cos_rows, precision=PRECISE) - jnp.einsum(
        "cxj,xi->cij", real_in, sin_rows, precision=PRECISE
    )
    return jnp.stack([coef_real, coef_imag])


def forward(values, row_positions, col_positions, row_length, col_length):
    return rows_transform(
        columns_transform(values, col_positions, col_length), row_positions, row_length
    )


def mix_modes(coeffs, weights):
    channels = coeffs.shape[1]
    flattened = coeffs.reshape(2, channels, MX * MY)
    weight_real = weights[0]
    weight_imag = weights[1]
    mixed_real = jnp.einsum(
        "koc,ck->ok", weight_real, flattened[0], precision=PRECISE
    ) - jnp.einsum("koc,ck->ok", weight_imag, flattened[1], precision=PRECISE)
    mixed_imag = jnp.einsum(
        "koc,ck->ok", weight_real, flattened[1], precision=PRECISE
    ) + jnp.einsum("koc,ck->ok", weight_imag, flattened[0], precision=PRECISE)
    return (mixed_real, mixed_imag)


def synthesis(mixed_real, mixed_imag, row_positions, col_positions, row_length, col_length):
    channels = mixed_real.shape[0]
    grid_real = mixed_real.reshape(channels, MX, MY)
    grid_imag = mixed_imag.reshape(channels, MX, MY)
    cos_rows, sin_rows = masked_table(row_positions, wave_numbers(), row_length)
    part_real = jnp.einsum("cij,xi->cxj", grid_real, cos_rows, precision=PRECISE) - jnp.einsum(
        "cij,xi->cxj", grid_imag, sin_rows, precision=PRECISE
    )
    part_imag = jnp.einsum("cij,xi->cxj", grid_real, sin_rows, precision=PRECISE) + jnp.einsum(
        "cij,xi->cxj", grid_imag, cos_rows, precision=PRECISE
    )
    cos_cols, sin_cols = masked_table(col_positions, jnp.arange(MY, dtype=jnp.int32), col_length)
    weight = jnp.where(jnp.arange(MY) == 0, 1.0, 2.0).astype(jnp.float32)
    lookup = jnp.concatenate(
        [(cos_cols * weight[None, :]).T, -(sin_cols * weight[None, :]).T], axis=0
    )
    stacked = jnp.concatenate([part_real, part_imag], axis=2)
    row_count = stacked.shape[1]
    result = jnp.dot(stacked.reshape(channels * row_count, 2 * MY), lookup, precision=PRECISE)
    return result.reshape(channels, row_count, col_positions.shape[0])


def finish_layer(
    coeffs, interior, own_mask, ext_rows, ext_cols, spec, w_point, b_point, w_in, w_out
):
    channels, tile_rows, tile_cols = interior.shape
    cell_count = tile_rows * tile_cols
    mixed_real, mixed_imag = mix_modes(coeffs, spec)
    spectral = synthesis(
        mixed_real,
        mixed_imag,
        H + jnp.arange(tile_rows, dtype=jnp.int32),
        H + jnp.arange(tile_cols, dtype=jnp.int32),
        ext_rows,
        ext_cols,
    )
    pre_act = (
        spectral.reshape(channels, cell_count)
        + jnp.dot(
            w_point, interior.reshape(channels, cell_count), preferred_element_type=jnp.float32
        )
        + b_point[:, None]
    )
    activated = jax.nn.gelu(pre_act, approximate=True).astype(jnp.bfloat16)
    hidden = jax.nn.gelu(
        jnp.dot(w_in, activated, preferred_element_type=jnp.float32), approximate=True
    ).astype(jnp.bfloat16)
    result = jnp.dot(w_out, hidden, preferred_element_type=jnp.float32) * own_mask.reshape(
        1, cell_count
    ).astype(jnp.float32)
    return result.reshape(channels, tile_rows, tile_cols).astype(jnp.bfloat16)


def fine_step(interior, own_mask, spec, w_point, b_point, w_in, w_out):
    channels, tile_rows, tile_cols = interior.shape
    ext_rows = tile_rows + 2 * H
    ext_cols = tile_cols + 2 * H
    extended = with_halo(interior, (("grp", 2), ("tile", 1)), H)
    coeffs = forward(
        extended,
        jnp.arange(ext_rows, dtype=jnp.int32),
        jnp.arange(ext_cols, dtype=jnp.int32),
        ext_rows,
        ext_cols,
    )
    coeffs = coeffs / (ext_rows * ext_cols)
    return finish_layer(
        coeffs, interior, own_mask, ext_rows, ext_cols, spec, w_point, b_point, w_in, w_out
    )


def local(
    ocean_state,
    sea_mask,
    spectral_weights,
    point_weights,
    point_bias,
    inner_weights,
    outer_weights,
    coarse_spectral,
    coarse_point,
    coarse_bias,
):
    channels, tile_rows, tile_cols = ocean_state.shape
    current = jnp.where(sea_mask[None] > 0, ocean_state, jnp.zeros((), jnp.bfloat16))
    for layer_index in range(LAYERS):
        current = fine_step(
            current,
            sea_mask,
            spectral_weights[layer_index],
            point_weights[layer_index],
            point_bias[layer_index],
            inner_weights[layer_index],
            outer_weights[layer_index],
        )
    fine_values = current.astype(jnp.float32)
    block_rows = tile_rows // R
    block_cols = tile_cols // R
    coarse = fine_values.reshape(channels, block_rows, R, block_cols, R).sum(axis=(2, 4)) / (R * R)
    grid_rows = block_rows * lax.axis_size("tile")
    grid_cols = block_cols * lax.axis_size("grp")
    row_positions = lax.axis_index("tile") * block_rows + jnp.arange(block_rows, dtype=jnp.int32)
    col_positions = lax.axis_index("grp") * block_cols + jnp.arange(block_cols, dtype=jnp.int32)
    slab_piece = lax.all_gather(coarse, "tile", axis=1, tiled=True)
    piece_rows = slab_piece.shape[1]
    y_modes = columns_transform(slab_piece, col_positions, grid_cols)
    partial_sum = rows_transform(y_modes, jnp.arange(piece_rows, dtype=jnp.int32), grid_rows)
    coeffs = lax.psum(partial_sum, "grp")
    coeffs = coeffs / (grid_rows * grid_cols)
    mixed_real, mixed_imag = mix_modes(coeffs, coarse_spectral)
    spectral = synthesis(mixed_real, mixed_imag, row_positions, col_positions, grid_rows, grid_cols)
    local_term = jnp.dot(
        coarse_point, coarse.reshape(channels, block_rows * block_cols), precision=PRECISE
    )
    correction = (
        spectral + local_term.reshape(channels, block_rows, block_cols) + coarse_bias[:, None, None]
    )
    land_sea = sea_mask.astype(jnp.float32).reshape(1, block_rows, R, block_cols, R)
    corrected = (
        fine_values.reshape(channels, block_rows, R, block_cols, R)
        + correction[:, :, None, :, None] * land_sea
    )
    return corrected.reshape(channels, tile_rows, tile_cols).astype(jnp.bfloat16)


def solution(mesh):
    placed = (P(None, "tile", "grp"), P("tile", "grp"), P(), P(), P(), P(), P(), P(), P(), P())
    return jax.shard_map(
        local, mesh=mesh, in_specs=placed, out_specs=P(None, "tile", "grp"), check_vma=False
    )
```

profile of v0, /device:TPU:1, one launch (start us, length us, event | category | flops | bytes accessed | tf_op | source)
XLA Modules:
  0.0 371.2 jit_solution(2826999524209507329)
XLA Ops:
  0.8 1.3 broadcast_select_fusion
  2.6 5.8 %collective-permute-start = (bf16[64,64,64]{2,1,0:T(8,128)(2,1)S(1)}, bf16[64,64,64]{2,1,0:T(8,128)(2,1)S(1)}, u32[]{:S(2)}, u32[]{:S(2)}) collective-permute-start(bf16[64,64,64]{2,1,0:T(8,128)(2,1)S(1)} %get-tuple-element.7), channel_id=1, source_target_pairs={{0,64},{64,128},{128,192},{1,65},{65,129},{129,193},{2,66},{66,130... | collective-permute-start | bytes 1572872 | tf_op jit(solution)/shard_map/ppermute | solution.py:25
  8.4 1.3 collective-permute-start.1
  9.7 20.5 %collective-permute-done = bf16[64,64,64]{2,1,0:T(8,128)(2,1)S(1)} collective-permute-done((bf16[64,64,64]{2,1,0:T(8,128)(2,1)S(1)}, bf16[64,64,64]{2,1,0:T(8,128)(2,1)S(1)}, u32[]{:S(2)}, u32[]{:S(2)}) %collective-permute-start) | collective-permute-done | bytes 524320 | tf_op jit(solution)/shard_map/ppermute | solution.py:25
  30.2 29.9 %collective-permute-done.1 = bf16[64,64,64]{2,1,0:T(8,128)(2,1)S(1)} collective-permute-done((bf16[64,64,64]{2,1,0:T(8,128)(2,1)S(1)}, bf16[64,64,64]{2,1,0:T(8,128)(2,1)S(1)}, u32[]{:S(2)}, u32[]{:S(2)}) %collective-permute-start.1) | collective-permute-done | bytes 524320 | tf_op jit(solution)/shard_map/ppermute | solution.py:26
  61.3 4.0 %collective-permute-start.2 = (bf16[64,64,256]{2,1,0:T(8,128)(2,1)S(1)}, bf16[64,64,256]{2,1,0:T(8,128)(2,1)S(1)}, u32[]{:S(2)}, u32[]{:S(2)}) collective-permute-start(bf16[64,64,256]{2,1,0:T(8,128)(2,1)S(1)} %pad_maximum_fusion), channel_id=1, source_target_pairs={{0,1},{1,2},{2,3},{3,4},{4,5},{5,6},{6,7},{7,8},{8,9},{9,10},{10,1... | collective-permute-start | bytes 6291464 | tf_op jit(solution)/shard_map/ppermute | solution.py:25
  65.4 2.1 collective-permute-start.3
  67.8 20.5 %collective-permute-done.2 = bf16[64,64,256]{2,1,0:T(8,128)(2,1)S(1)} collective-permute-done((bf16[64,64,256]{2,1,0:T(8,128)(2,1)S(1)}, bf16[64,64,256]{2,1,0:T(8,128)(2,1)S(1)}, u32[]{:S(2)}, u32[]{:S(2)}) %collective-permute-start.2) | collective-permute-done | bytes 2097184 | tf_op jit(solution)/shard_map/ppermute | solution.py:25
  88.3 4.4 %collective-permute-done.3 = bf16[64,64,256]{2,1,0:T(8,128)(2,1)S(1)} collective-permute-done((bf16[64,64,256]{2,1,0:T(8,128)(2,1)S(1)}, bf16[64,64,256]{2,1,0:T(8,128)(2,1)S(1)}, u32[]{:S(2)}, u32[]{:S(2)}) %collective-permute-start.3) | collective-permute-done | bytes 2097184 | tf_op jit(solution)/shard_map/ppermute | solution.py:26
  92.7 5.1 %fusion.8 = f32[64,192,8]{1,2,0:T(8,128)S(1)} fusion(bf16[64,64,256]{2,1,0:T(8,128)(2,1)S(1)} %collective-permute-done.3, bf16[64,64,64]{2,1,0:T(8,128)(2,1)S(1)} %collective-permute-done.1, bf16[64,64,128]{2,1,0:T(8,128)(2,1)S(1)} %broadcast_select_fusion, bf16[64,64,64]{2,1,0:T(8,128)(2,1)S(1)} %collective-permute-done, ...), kind=kOutput, calls=%fused_computation.14 | convolution fusion | flops 333449216 | bytes 6692864 | tf_op jit(solution)/shard_map/dot_general | solution.py:48
  100.0 1.7 fusion.92
  101.7 1.7 fusion.98
  103.5 1.7 fusion.96
  105.2 1.7 fusion.94
  109.1 3.7 fusion.273
  112.8 1.6 reshape_reshape.6
  114.3 3.1 fusion.51
  117.4 1.8 fusion.4
  120.0 5.4 %collective-permute-start.4 = (bf16[64,64,64]{2,1,0:T(8,128)(2,1)S(1)}, bf16[64,64,64]{2,1,0:T(8,128)(2,1)S(1)}, u32[]{:S(2)}, u32[]{:S(2)}) collective-permute-start(bf16[64,64,64]{2,1,0:T(8,128)(2,1)S(1)} %get-tuple-element.5), channel_id=1, source_target_pairs={{0,64},{64,128},{128,192},{1,65},{65,129},{129,193},{2,66},{66,130... | collective-permute-start | bytes 1572872 | tf_op jit(solution)/shard_map/ppermute | solution.py:25
  125.4 1.3 collective-permute-start.5
  126.7 10.4 %collective-permute-done.4 = bf16[64,64,64]{2,1,0:T(8,128)(2,1)S(1)} collective-permute-done((bf16[64,64,64]{2,1,0:T(8,128)(2,1)S(1)}, bf16[64,64,64]{2,1,0:T(8,128)(2,1)S(1)}, u32[]{:S(2)}, u32[]{:S(2)}) %collective-permute-start.4) | collective-permute-done | bytes 524320 | tf_op jit(solution)/shard_map/ppermute | solution.py:25
  137.1 25.0 %collective-permute-done.5 = bf16[64,64,64]{2,1,0:T(8,128)(2,1)S(1)} collective-permute-done((bf16[64,64,64]{2,1,0:T(8,128)(2,1)S(1)}, bf16[64,64,64]{2,1,0:T(8,128)(2,1)S(1)}, u32[]{:S(2)}, u32[]{:S(2)}) %collective-permute-start.5) | collective-permute-done | bytes 524320 | tf_op jit(solution)/shard_map/ppermute | solution.py:26
  162.1 1.3 pad_maximum_fusion.1
  163.5 14.2 %collective-permute-start.6 = (bf16[64,64,256]{2,1,0:T(8,128)(2,1)S(1)}, bf16[64,64,256]{2,1,0:T(8,128)(2,1)}, u32[]{:S(2)}, u32[]{:S(2)}) collective-permute-start(bf16[64,64,256]{2,1,0:T(8,128)(2,1)S(1)} %pad_maximum_fusion.1), channel_id=1, source_target_pairs={{0,1},{1,2},{2,3},{3,4},{4,5},{5,6},{6,7},{7,8},{8,9},{9,10},{10,1... | collective-permute-start | bytes 6291464 | tf_op jit(solution)/shard_map/ppermute | solution.py:25
  177.7 2.4 collective-permute-start.7
  180.3 20.3 %collective-permute-done.6 = bf16[64,64,256]{2,1,0:T(8,128)(2,1)} collective-permute-done((bf16[64,64,256]{2,1,0:T(8,128)(2,1)S(1)}, bf16[64,64,256]{2,1,0:T(8,128)(2,1)}, u32[]{:S(2)}, u32[]{:S(2)}) %collective-permute-start.6) | collective-permute-done | bytes 2097184 | tf_op jit(solution)/shard_map/ppermute | solution.py:25
  200.6 4.5 %collective-permute-done.7 = bf16[64,64,256]{2,1,0:T(8,128)(2,1)} collective-permute-done((bf16[64,64,256]{2,1,0:T(8,128)(2,1)S(1)}, bf16[64,64,256]{2,1,0:T(8,128)(2,1)}, u32[]{:S(2)}, u32[]{:S(2)}) %collective-permute-start.7) | collective-permute-done | bytes 2097184 | tf_op jit(solution)/shard_map/ppermute | solution.py:26
  205.1 7.6 %fusion.18 = f32[64,192,8]{1,2,0:T(8,128)S(1)} fusion(bf16[64,64,256]{2,1,0:T(8,128)(2,1)} %collective-permute-done.7, bf16[64,64,64]{2,1,0:T(8,128)(2,1)} %copy-done.6, bf16[64,64,128]{2,1,0:T(8,128)(2,1)S(1)} %bitcast.319, bf16[64,64,64]{2,1,0:T(8,128)(2,1)} %copy-done.5, bf16[64,64,256]{2,1,0:T(8,128)(2,1)} %collective-permute-done.6, ...), kind=kOutput, calls=%fused_computation.24 | convolution fusion | flops 333449216 | bytes 6692864 | tf_op jit(solution)/shard_map/dot_general | solution.py:48
  214.9 1.7 fusion.84
  216.6 1.7 fusion.90
  218.4 1.7 fusion.88
  220.1 1.7 fusion.86
  224.0 3.4 fusion.272
  227.4 1.7 reshape_reshape.7
  229.1 3.6 fusion.59
  232.8 3.0 fusion.7
  235.8 2.8 copy.156
  238.6 2.6 reduce_sum.9
  241.2 83.6 %all_gather.3 = f32[64,256,8]{0,2,1:T(8,128)S(1)} all-gather(f32[64,4,8]{0,2,1:T(8,128)S(1)} %broadcast_multiply_fusion.1), channel_id=1, replica_groups=mesh['grp'=4,'tile'=64] {'tile'}, dimensions={1}, use_global_device_ids=true | all-gather | bytes 532480 | tf_op jit(solution)/shard_map/all_gather | solution.py:189
  324.8 7.4 %copy.116 = f32[64,256,8]{2,1,0:T(8,128)} copy(f32[64,256,8]{0,2,1:T(8,128)S(1)} %all_gather.3) | data formatting | bytes 1048576 | tf_op jit(solution)/shard_map/all_gather | solution.py:189
  332.2 9.8 %fusion.201 = f32[64,256,8]{1,2,0:T(8,128)S(1)} fusion(f32[64,256,8]{2,1,0:T(8,128)} %copy.116, f32[8,4]{0,1:T(4,128)S(1)} %get-tuple-element.28, f32[8,4]{0,1:T(4,128)S(1)} %get-tuple-element.27), kind=kOutput, calls=%fused_computation.257 | convolution fusion | flops 12582976 | bytes 1048832 | tf_op jit(solution)/shard_map/dot_general | solution.py:48
  344.1 13.8 %psum.7 = f32[2,64,8,4]{1,2,3,0:T(8,128)S(1)} all-reduce(f32[2,64,8,4]{1,2,3,0:T(8,128)S(1)} %pad_maximum_fusion.4), channel_id=1, replica_groups=mesh['grp'=4,'tile'=64] {'grp'}, use_global_device_ids=true, to_apply=%region_1.2 | all-reduce | flops 4096 | bytes 32768 | tf_op jit(solution)/shard_map/psum | solution.py:193
  357.9 1.7 fusion.80
  359.6 1.7 fusion.78
  361.4 1.7 fusion.76
  363.1 1.7 fusion.82
  367.1 1.5 add_convert_fusion
  368.6 2.3 copy.133
  (110 shorter events, 16.4 us)
Async XLA Ops:
  0.0 366.4 %copy-start = (f32[64,64]{1,0:T(8,128)S(1)}, f32[64,64]{1,0:T(8,128)}, u32[]{:S(2)}) copy-start(f32[64,64]{1,0:T(8,128)} %param.18) | copy-start | bytes 49156
  2.1 65.5 %copy-start.10 = (f32[2,64]{1,0:T(2,128)S(1)}, f32[2,64]{1,0:T(2,128)}, u32[]{:S(2)}) copy-start(f32[2,64]{1,0:T(2,128)} %param.14) | copy-start | bytes 1540
  2.1 65.7 %copy-start.9 = (s32[64,128]{1,0:T(8,128)S(1)}, s32[64,128]{1,0:T(8,128)}, u32[]{:S(2)}) copy-start(s32[64,128]{1,0:T(8,128)} %param.11) | copy-start | bytes 98308
  2.6 27.6 %collective-permute-start = (bf16[64,64,64]{2,1,0:T(8,128)(2,1)S(1)}, bf16[64,64,64]{2,1,0:T(8,128)(2,1)S(1)}, u32[]{:S(2)}, u32[]{:S(2)}) collective-permute-start(bf16[64,64,64]{2,1,0:T(8,128)(2,1)S(1)} %get-tuple-element.7), channel_id=1, source_target_pairs={{0,64},{64,128},{128,192},{1,65},{65,129},{129,193},{2,66},{66,130... | collective-permute-start | bytes 1572872 | tf_op jit(solution)/shard_map/ppermute | solution.py:25
  8.4 51.7 %collective-permute-start.1 = (bf16[64,64,64]{2,1,0:T(8,128)(2,1)S(1)}, bf16[64,64,64]{2,1,0:T(8,128)(2,1)S(1)}, u32[]{:S(2)}, u32[]{:S(2)}) collective-permute-start(bf16[64,64,64]{2,1,0:T(8,128)(2,1)S(1)} %get-tuple-element.8), channel_id=1, source_target_pairs={{64,0},{128,64},{192,128},{65,1},{129,65},{193,129},{66,2},{130,66... | collective-permute-start | bytes 1572872 | tf_op jit(solution)/shard_map/ppermute | solution.py:26
  61.3 27.0 %collective-permute-start.2 = (bf16[64,64,256]{2,1,0:T(8,128)(2,1)S(1)}, bf16[64,64,256]{2,1,0:T(8,128)(2,1)S(1)}, u32[]{:S(2)}, u32[]{:S(2)}) collective-permute-start(bf16[64,64,256]{2,1,0:T(8,128)(2,1)S(1)} %pad_maximum_fusion), channel_id=1, source_target_pairs={{0,1},{1,2},{2,3},{3,4},{4,5},{5,6},{6,7},{7,8},{8,9},{9,10},{10,1... | collective-permute-start | bytes 6291464 | tf_op jit(solution)/shard_map/ppermute | solution.py:25
  65.4 27.4 %collective-permute-start.3 = (bf16[64,64,256]{2,1,0:T(8,128)(2,1)S(1)}, bf16[64,64,256]{2,1,0:T(8,128)(2,1)S(1)}, u32[]{:S(2)}, u32[]{:S(2)}) collective-permute-start(bf16[64,64,256]{2,1,0:T(8,128)(2,1)S(1)} %pad_maximum_fusion), channel_id=1, source_target_pairs={{1,0},{2,1},{3,2},{4,3},{5,4},{6,5},{7,6},{8,7},{9,8},{10,9},{11,1... | collective-permute-start | bytes 6291464 | tf_op jit(solution)/shard_map/ppermute | solution.py:26
  92.7 7.2 %copy-start.2 = (f32[2,2,32,64,64]{4,3,2,1,0:T(8,128)S(1)}, f32[2,2,32,64,64]{4,3,2,1,0:T(8,128)}, u32[]{:S(2)}) copy-start(f32[2,2,32,64,64]{4,3,2,1,0:T(8,128)} %param.12) | copy-start | bytes 6291460
  107.9 6.4 %copy-start.12 = (bf16[2,64,64]{2,1,0:T(8,128)(2,1)S(1)}, bf16[2,64,64]{2,1,0:T(8,128)(2,1)}, u32[]{:S(2)}) copy-start(bf16[2,64,64]{2,1,0:T(8,128)(2,1)} %param.13) | copy-start | bytes 49156
  114.3 3.1 copy-start.13
  114.3 3.1 copy-start.14
  119.2 17.9 %copy-start.7 = (bf16[8192,64]{0,1:T(8,128)(2,1)}, bf16[8192,64]{0,1:T(8,128)(2,1)S(1)}, u32[]{:S(2)}) copy-start(bf16[8192,64]{0,1:T(8,128)(2,1)S(1)} %fusion.4) | copy-start | bytes 3145732
  120.0 17.1 %collective-permute-start.4 = (bf16[64,64,64]{2,1,0:T(8,128)(2,1)S(1)}, bf16[64,64,64]{2,1,0:T(8,128)(2,1)S(1)}, u32[]{:S(2)}, u32[]{:S(2)}) collective-permute-start(bf16[64,64,64]{2,1,0:T(8,128)(2,1)S(1)} %get-tuple-element.5), channel_id=1, source_target_pairs={{0,64},{64,128},{128,192},{1,65},{65,129},{129,193},{2,66},{66,130... | collective-permute-start | bytes 1572872 | tf_op jit(solution)/shard_map/ppermute | solution.py:25
  125.4 36.7 %collective-permute-start.5 = (bf16[64,64,64]{2,1,0:T(8,128)(2,1)S(1)}, bf16[64,64,64]{2,1,0:T(8,128)(2,1)S(1)}, u32[]{:S(2)}, u32[]{:S(2)}) collective-permute-start(bf16[64,64,64]{2,1,0:T(8,128)(2,1)S(1)} %get-tuple-element.6), channel_id=1, source_target_pairs={{64,0},{128,64},{192,128},{65,1},{129,65},{193,129},{66,2},{130,66... | collective-permute-start | bytes 1572872 | tf_op jit(solution)/shard_map/ppermute | solution.py:26
  137.1 42.9 %copy-start.5 = (bf16[64,64,64]{2,1,0:T(8,128)(2,1)}, bf16[64,64,64]{2,1,0:T(8,128)(2,1)S(1)}, u32[]{:S(2)}) copy-start(bf16[64,64,64]{2,1,0:T(8,128)(2,1)S(1)} %collective-permute-done.4) | copy-start | bytes 1572868
  162.1 17.9 %copy-start.6 = (bf16[64,64,64]{2,1,0:T(8,128)(2,1)}, bf16[64,64,64]{2,1,0:T(8,128)(2,1)S(1)}, u32[]{:S(2)}) copy-start(bf16[64,64,64]{2,1,0:T(8,128)(2,1)S(1)} %collective-permute-done.5) | copy-start | bytes 1572868
  163.5 37.1 %collective-permute-start.6 = (bf16[64,64,256]{2,1,0:T(8,128)(2,1)S(1)}, bf16[64,64,256]{2,1,0:T(8,128)(2,1)}, u32[]{:S(2)}, u32[]{:S(2)}) collective-permute-start(bf16[64,64,256]{2,1,0:T(8,128)(2,1)S(1)} %pad_maximum_fusion.1), channel_id=1, source_target_pairs={{0,1},{1,2},{2,3},{3,4},{4,5},{5,6},{6,7},{7,8},{8,9},{9,10},{10,1... | collective-permute-start | bytes 6291464 | tf_op jit(solution)/shard_map/ppermute | solution.py:25
  177.7 27.5 %collective-permute-start.7 = (bf16[64,64,256]{2,1,0:T(8,128)(2,1)S(1)}, bf16[64,64,256]{2,1,0:T(8,128)(2,1)}, u32[]{:S(2)}, u32[]{:S(2)}) collective-permute-start(bf16[64,64,256]{2,1,0:T(8,128)(2,1)S(1)} %pad_maximum_fusion.1), channel_id=1, source_target_pairs={{1,0},{2,1},{3,2},{4,3},{5,4},{6,5},{7,6},{8,7},{9,8},{10,9},{11,1... | collective-permute-start | bytes 6291464 | tf_op jit(solution)/shard_map/ppermute | solution.py:26
  180.3 34.6 %copy-start.3 = (f32[2,2,32,64,64]{4,3,2,1,0:T(8,128)S(1)}, f32[2,2,32,64,64]{4,3,2,1,0:T(8,128)}, u32[]{:S(2)}) copy-start(f32[2,2,32,64,64]{4,3,2,1,0:T(8,128)} %param.12) | copy-start | bytes 6291460
  222.8 6.3 %copy-start.8 = (bf16[8192,64]{0,1:T(8,128)(2,1)S(1)}, bf16[8192,64]{0,1:T(8,128)(2,1)}, u32[]{:S(2)}) copy-start(bf16[8192,64]{0,1:T(8,128)(2,1)} %copy-done.7) | copy-start | bytes 3145732
  332.2 25.7 %copy-start.4 = (f32[2,32,64,64]{3,2,1,0:T(8,128)S(1)}, f32[2,32,64,64]{3,2,1,0:T(8,128)}, u32[]{:S(2)}) copy-start(f32[2,32,64,64]{3,2,1,0:T(8,128)} %param.17) | copy-start | bytes 3145732
  341.9 24.5 %copy-start.11 = (f32[64]{0:T(128)S(1)}, f32[64]{0:T(128)}, u32[]{:S(2)}) copy-start(f32[64]{0:T(128)} %param.19) | copy-start | bytes 772
  359.6 7.5 %copy-start.1 = (f32[64,8192]{0,1:T(8,128)S(1)}, f32[64,8192]{0,1:T(8,128)}, u32[]{:S(2)}) copy-start(f32[64,8192]{0,1:T(8,128)} %copy.156) | copy-start | bytes 6291460
where the time goes:
time: 376 us; the launch traced here: 371 us
  waiting for transfers between devices  136 us (36%)
  blocking collectives  97.3 us (26%)
  matrix products  73.2 us (19%)
  starting transfers between devices  36.5 us (10%)
  local copies, waits for them, and re-layouts  18.3 us (5%)
  other arithmetic  9.35 us (2%)
    all_gather x1, blocking collectives, local(): slab_piece = lax.all_gather(coarse, 'tile', axis=1, tiled=True)  83.6 us
    ppermute x4, waiting for transfers between devices, with_halo(): before = lax.ppermute(last, axis, up)  71.7 us
    ppermute x4, waiting for transfers between devices, with_halo(): after = lax.ppermute(first, axis, down)  63.8 us
    ppermute x4, starting transfers between devices, with_halo(): before = lax.ppermute(last, axis, up)  29.4 us
    dot_general x3, matrix products, columns_transform(): jnp.dot(flattened, lookup, precision=PRECISE, preferred_element_type=jnp....  22.5 us
    psum x1, blocking collectives, local(): coeffs = lax.psum(partial_sum, 'grp')  13.8 us
  transfers between devices with their start and end apart: 8, of which 8 were waited for; matrix products, arithmetic and copies ran while one was open for 0% of the time, Pallas kernels for 0%

commit v1 on v0

v1 whole, which is shorter than its diff:
```python
import functools
import math

import jax
import jax.numpy as jnp
import numpy as np
from jax import lax
from jax.experimental import pallas as pl
from jax.experimental.pallas import tpu as pltpu
from jax.sharding import PartitionSpec as P

MESH = pl.DeviceIdType.MESH
F32 = jnp.float32
BF16 = jnp.bfloat16
PRECISE = lax.Precision.HIGHEST

C = 64
F = 128
TX = 64
TY = 128
L1 = 192
L2 = 256
NT = 64
NG = 4
PAD = 72
GROUPS = 8
GELU0 = math.sqrt(2.0 / math.pi)
GELU1 = GELU0 * 0.044715


def lane_numbers():
    lane = np.arange(128)
    ri, half, k = lane // 64, (lane // 32) % 2, lane % 32
    i, j = k // 4, k % 4
    kappa = np.where(i < 4, i, i - 8)
    return ri, half, kappa, j


def constants():
    ri, half, kappa, j = lane_numbers()
    two_pi = 2.0 * np.pi
    cell = np.arange(1024)
    b, q = cell // 128, cell % 128

    phi = two_pi * (b[:, None] * kappa / L1 + (q % 64)[:, None] * j / L2)
    table = np.where(ri == 0, np.cos(phi), -np.sin(phi)) * ((q // 64)[:, None] == half)

    rows = np.arange(64)
    ri_r, k_r = rows // 32, rows % 32
    i_r, j_r = k_r // 4, k_r % 4
    kap_r = np.where(i_r < 4, i_r, i_r - 8)
    phi = two_pi * (kap_r[:, None] * (64 + b) / L1 + j_r[:, None] * (64 + q) / L2)
    basis = np.where(ri_r[:, None] == 0, np.cos(phi), -np.sin(phi))

    pool = ((np.arange(128) % 8)[None, :] == (q // 16)[:, None]) & (np.arange(128) < 32)[None, :]

    def forward(theta):
        return np.cos(theta), np.where(ri == 0, 1.0, -1.0) * np.sin(theta)

    weight = np.where(j == 0, 1.0, 2.0)
    rot = []
    for a in range(GROUPS):
        rot += list(forward(two_pi * kappa * a / 24))
    for rho in range(3):
        rot += list(forward(two_pi * kappa * rho / 3))
    rot += list(forward(two_pi * j * np.where(half == 0, 1, 2) / 4))
    rot += list(forward(two_pi * j * np.where(half == 0, 3, 0) / 4))
    for a in range(GROUPS):
        cos, sin = forward(two_pi * kappa * a / 24)
        rot += [cos * weight / (L1 * L2), -sin * weight / (L1 * L2)]
    rot = np.stack(rot)
    rot = np.concatenate([rot, np.zeros((48 - rot.shape[0], 128))])

    small = np.arange(128)
    br, bq = small // 8, small % 8
    theta = two_pi * (br[:, None] * kappa / 256 + bq[:, None] * j / 32)
    ctab = np.where(ri == 0, np.cos(theta), -np.sin(theta)) * (small < 32)[:, None]
    wide = np.arange(512)
    wr, wq = wide // 128, (wide % 128) // 16
    theta = two_pi * (kappa[:, None] * wr / 256 + j[:, None] * wq / 32)
    stab = np.where(ri[:, None] == 0, np.cos(theta), -np.sin(theta)) * weight[:, None] / (256 * 32)
    stab = stab * (half == 0)[:, None]
    spread = ((br[:, None] == wr) & (bq[:, None] == wq) & (small < 32)[:, None])

    place = np.zeros((64, 128))
    for c in range(64):
        place[c, (32 + c) if c < 32 else (64 + c)] = 1.0

    dev = np.zeros((NT * NG, 2, 128))
    for t in range(NT):
        for g in range(NG):
            dev[t * NG + g, 0], dev[t * NG + g, 1] = forward(two_pi * ((kappa * t % 64) / 64 + (j * g % 4) / 4))
    return dict(
        table=table.astype(BF16),
        basis=basis.astype(BF16),
        pool=pool.astype(np.float32).astype(BF16),
        rot=rot.astype(np.float32),
        ctab=ctab.astype(np.float32),
        stab=stab.astype(np.float32),
        spread=spread.astype(np.float32),
        place=place.astype(BF16),
        dev=dev.astype(np.float32),
    )


ROW3, OWN, REC, SYN = 16, 22, 24, 26


def gelu(v):
    half = 0.5 * v
    return half + half * jnp.tanh(v * (GELU0 + GELU1 * (v * v)))


def dot(a, b):
    return jnp.dot(a, b, preferred_element_type=F32)


def exact(a, b):
    return jnp.dot(a, b, precision=PRECISE, preferred_element_type=F32)


def kernel(
    x_ref, mask_ref, w_ref, wp_ref, bp_ref, win_ref, wout_ref, wc_ref, cp_ref, cb_ref,
    table, basis, pool, rot, ctab, stab, spread, place, dev_ref,
    out_ref,
    xs, mf, fa, fb, wv, lhs, wpad, bias, pbuf, vrecv, hsend, hrecv, csend, crecv, local, cx, devv,
    wsem, ssem, rsem,
):
    t = lax.axis_index("tile")
    g = lax.axis_index("grp")

    weights = [pltpu.make_async_copy(w_ref.at[l], wv.at[l], wsem.at[l]) for l in range(2)]
    weights.append(pltpu.make_async_copy(wc_ref, wv.at[2], wsem.at[2]))
    phase = pltpu.make_async_copy(dev_ref.at[t * NG + g], devv, wsem.at[3])
    for copy in weights:
        copy.start()
    phase.start()

    def at(tile, grp):
        return {"tile": tile, "grp": grp}

    up, down = at(lax.rem(t + NT - 1, NT), g), at(lax.rem(t + 1, NT), g)
    left, right = at(t, lax.rem(g + NG - 1, NG)), at(t, lax.rem(g + 1, NG))
    yc, xc = lax.rem(t, 8), lax.div(t, 16)
    zc = 2 * g + lax.rem(lax.div(t, 8), 2)
    flat = [at(t - yc + lax.rem(yc + d, 8), g) for d in range(1, 8)]
    along_x = [at(lax.rem(xc + d, 4) * 16 + lax.rem(t, 16), g) for d in range(1, 4)]
    along_z = []
    for d in range(1, 8):
        z = lax.rem(zc + d, 8)
        along_z.append(at(xc * 16 + lax.rem(z, 2) * 8 + yc, lax.div(z, 2)))

    barrier = pltpu.get_barrier_semaphore()
    partners = [up, down, left, right] + flat + along_x + along_z
    for partner in partners:
        pl.semaphore_signal(barrier, inc=1, device_id=partner, device_id_type=MESH)

    lane = lax.broadcasted_iota(jnp.int32, (64, 128), 1)
    mode = lane % 32
    in_a = (lane // 32) % 2 == 0
    in_a32 = in_a[:32]
    re_sign = jnp.where(lane < 64, -1.0, 1.0).astype(F32)

    def turned(v, row):
        return v * rot[row : row + 1, :] + pltpu.roll(v, 64, 1) * rot[row + 1 : row + 2, :]

    mf[...] = mask_ref[...].astype(F32)

    def mask_step(c, carry):
        xs[pl.ds(pl.multiple_of(c * PAD, 8), 64), :] = jnp.where(mask_ref[...] > 0, x_ref[c].astype(F32), 0.0)
        return carry

    lax.fori_loop(0, C, mask_step, 0, unroll=4)

    def analysis(field, a, total):
        part = dot(field[a], table[...])
        cos = rot[pl.ds(2 * a, 1), :]
        sin = rot[pl.ds(2 * a + 1, 1), :]
        return total + part * cos + pltpu.roll(part, 64, 1) * sin

    def group_step(a, total):
        for b in range(8):
            fa[a, :, b * 128 : (b + 1) * 128] = xs[pl.ds(8 * a + b, 64, stride=PAD), :].astype(BF16)
        return analysis(fa, a, total)

    total = lax.fori_loop(0, GROUPS, group_step, jnp.zeros((64, 128), F32))

    eye = lax.broadcasted_iota(jnp.int32, (64, 64), 0) == lax.broadcasted_iota(jnp.int32, (64, 64), 1)

    def column(row):
        return jnp.broadcast_to(jnp.sum(jnp.where(eye, row, 0.0), axis=1, keepdims=True), (64, 128))

    for l in range(2):
        wpad[l] = dot(wp_ref[l], place[...])
        bias[l] = column(bp_ref[l : l + 1, :])
    bias[2] = column(cb_ref[...])

    def remote(src, dst, number, device):
        return pltpu.make_async_remote_copy(
            src_ref=src, dst_ref=dst, send_sem=ssem.at[number], recv_sem=rsem.at[number],
            device_id=device, device_id_type=MESH,
        )

    def exchange(l, total):
        pbuf[l] = total
        sends = [
            remote(pbuf.at[l], vrecv.at[l, 1], 4 * l, up),
            remote(pbuf.at[l], vrecv.at[l, 0], 4 * l + 1, down),
        ]
        for s in sends:
            s.start()
        own = turned(total, ROW3 + 2)
        for s in sends:
            s.wait()
        above = jnp.where(t > 0, vrecv[l, 0], 0.0)
        below = jnp.where(t < NT - 1, vrecv[l, 1], 0.0)
        v = own + turned(above, ROW3) + turned(below, ROW3 + 4)
        hsend[l, 0] = jnp.where(in_a32, v[:32], pltpu.roll(v[32:], 32, 1))
        hsend[l, 1] = jnp.where(in_a32, pltpu.roll(v[:32], 96, 1), v[32:])
        sends = [
            remote(hsend.at[l, 0], hrecv.at[l, 0], 4 * l + 2, left),
            remote(hsend.at[l, 1], hrecv.at[l, 1], 4 * l + 3, right),
        ]
        for s in sends:
            s.start()
        own = turned(v, OWN)
        for s in sends:
            s.wait()
        from_right = jnp.where(g < NG - 1, hrecv[l, 0], 0.0)
        from_left = jnp.where(g > 0, hrecv[l, 1], 0.0)
        first = jnp.concatenate([from_right, pltpu.roll(from_right, 96, 1)], axis=0)
        second = jnp.concatenate([pltpu.roll(from_left, 32, 1), from_left], axis=0)
        both = own + turned(jnp.where(in_a, first, second), REC)
        return both + pltpu.roll(both, 96, 1)

    def mix(l, u):
        plain = u.astype(BF16)
        crossed = (pltpu.roll(u, 64, 1) * re_sign).astype(BF16)
        acc = jnp.zeros((64, 128), F32)
        for block in range(8):
            rows = slice(block * 256, (block + 1) * 256)
            o = dot(wv[l, 0, rows, :].astype(BF16), plain) + dot(wv[l, 1, rows, :].astype(BF16), crossed)
            for n in range(4):
                acc = acc + jnp.where(mode == block * 4 + n, o[n * 64 : (n + 1) * 64], 0.0)
        return acc

    def layer(l, src, dst, v, per_group, start):
        for a in range(GROUPS):
            lhs[a] = jnp.where(in_a, turned(v, SYN + 2 * a), wpad[l]).astype(BF16)

        def step(a, total):
            for n in range(4):
                cols = slice(n * 256, (n + 1) * 256)
                rhs = jnp.concatenate(
                    [basis[:32, cols], src[a, :32, cols], basis[32:, cols], src[a, 32:, cols]], axis=0
                )
                shift = jnp.concatenate([bias[l], bias[l]], axis=1)
                act = gelu(dot(lhs[a], rhs) + shift).astype(BF16)
                hid = gelu(dot(win_ref[l], act)).astype(BF16)
                sea = jnp.concatenate(
                    [mf[pl.ds(8 * a + 2 * n, 1), :], mf[pl.ds(8 * a + 2 * n + 1, 1), :]], axis=1
                )
                dst[a, :, cols] = (dot(wout_ref[l], hid) * sea).astype(BF16)
            return per_group(dst, a, total)

        return lax.fori_loop(0, GROUPS, step, start)

    pl.semaphore_wait(barrier, len(partners))
    u = exchange(0, total)
    weights[0].wait()
    v = mix(0, u)
    total = layer(0, fa, fb, v, analysis, jnp.zeros((64, 128), F32))
    u = exchange(1, total)
    weights[1].wait()
    v = mix(1, u)

    def pooled(field, a, total):
        return total + jnp.where(lane // 8 == a // 2, dot(field[a], pool[...]), 0.0)

    coarse = layer(1, fb, fa, v, pooled, jnp.zeros((64, 128), F32)) * (1.0 / 256.0)

    phase.wait()
    cos, sin = devv[0:1, :], devv[1:2, :]
    part = exact(coarse, ctab[...])
    part = part * cos + pltpu.roll(part, 64, 1) * sin
    acc = jnp.where(in_a32, part[:32], part[32:])
    number, slot = 8, 0
    for stage, peers in enumerate((flat, along_x, along_z)):
        csend[stage] = acc
        sends = []
        for peer in peers:
            sends.append(remote(csend.at[stage], crecv.at[slot], number, peer))
            number, slot = number + 1, slot + 1
        for s in sends:
            s.start()
        if stage == 0:
            local[...] = exact(cp_ref[...], exact(coarse, spread[...])) + jnp.concatenate([bias[2]] * 4, axis=1)
        if stage == 2:
            def back_step(a, carry):
                for b in range(8):
                    xs[pl.ds(8 * a + b, 64, stride=PAD), :] = fa[a, :, b * 128 : (b + 1) * 128].astype(F32)
                return carry

            lax.fori_loop(0, GROUPS, back_step, 0)
        for s in sends:
            s.wait()
        for n in range(slot - len(peers), slot):
            acc = acc + crecv[n]
    u = jnp.concatenate([acc, pltpu.roll(acc, 96, 1)], axis=0)
    weights[2].wait()
    v = mix(2, u)
    v = v * cos - pltpu.roll(v, 64, 1) * sin
    full = exact(jnp.where(in_a, v, 0.0), stab[...]) + local[...]
    for n in range(4):
        cx[n] = full[:, n * 128 : (n + 1) * 128]

    def final_step(c, carry):
        rows = []
        for n in range(4):
            fix = jnp.broadcast_to(cx[n, pl.ds(c, 1), :], (16, 128))
            base = pl.multiple_of(c * PAD, 8)
            rows.append(xs[pl.ds(base + 16 * n, 16), :] + fix * mf[16 * n : 16 * (n + 1), :])
        out_ref[c] = jnp.concatenate(rows, axis=0).astype(BF16)
        return carry

    lax.fori_loop(0, C, final_step, 0, unroll=2)


def local_program(consts, x, mask, w, wp, bp, win, wout, wc, cp, cb):
    vmem = pl.BlockSpec(memory_space=pltpu.VMEM)
    hbm = pl.BlockSpec(memory_space=pl.ANY)
    n_remote = 8 + 17
    return pl.pallas_call(
        kernel,
        out_shape=jax.ShapeDtypeStruct((C, TX, TY), BF16),
        in_specs=[vmem, vmem, hbm, vmem, vmem, vmem, vmem, hbm, vmem, vmem] + [vmem] * 8 + [hbm],
        out_specs=vmem,
        scratch_shapes=[
            pltpu.VMEM((C * PAD, 128), F32),
            pltpu.VMEM((TX, TY), F32),
            pltpu.VMEM((GROUPS, C, 1024), BF16),
            pltpu.VMEM((GROUPS, C, 1024), BF16),
            pltpu.VMEM((3, 2, 2048, 64), F32),
            pltpu.VMEM((GROUPS, C, 128), BF16),
            pltpu.VMEM((2, C, 128), F32),
            pltpu.VMEM((3, C, 128), F32),
            pltpu.VMEM((2, C, 128), F32),
            pltpu.VMEM((2, 2, C, 128), F32),
            pltpu.VMEM((2, 2, 32, 128), F32),
            pltpu.VMEM((2, 2, 32, 128), F32),
            pltpu.VMEM((3, 32, 128), F32),
            pltpu.VMEM((17, 32, 128), F32),
            pltpu.VMEM((C, 512), F32),
            pltpu.VMEM((4, C, 128), F32),
            pltpu.VMEM((2, 128), F32),
            pltpu.SemaphoreType.DMA((4,)),
            pltpu.SemaphoreType.DMA((n_remote,)),
            pltpu.SemaphoreType.DMA((n_remote,)),
        ],
        compiler_params=pltpu.CompilerParams(
            collective_id=0, has_side_effects=True, vmem_limit_bytes=48 * 1024 * 1024
        ),
        name="ocean",
    )(
        x, mask, w.reshape(2, 2, 2048, 64), wp, bp, win, wout, wc.reshape(2, 2048, 64), cp, cb.reshape(1, 64),
        consts["table"], consts["basis"], consts["pool"], consts["rot"], consts["ctab"], consts["stab"],
        consts["spread"], consts["place"], consts["dev"],
    )


def solution(mesh):
    consts = constants()

    def body(*args):
        return local_program({k: jnp.asarray(v) for k, v in consts.items()}, *args)

    placed = (P(None, "tile", "grp"), P("tile", "grp"), P(), P(), P(), P(), P(), P(), P(), P())
    return jax.shard_map(body, mesh=mesh, in_specs=placed, out_specs=P(None, "tile", "grp"), check_vma=False)
```

time: 376 us -> 81.6 us (0.22); the launches traced: 371 us -> 80.8 us
  waiting for transfers between devices: 136 us -> 0 us
  blocking collectives: 97.3 us -> 0 us
  matrix products: 73.2 us -> 0 us
  Pallas kernels: 0 us -> 63.8 us
  starting transfers between devices: 36.5 us -> 0 us
  other arithmetic: 9.35 us -> 0 us
    ppermute x8 -> x0, waiting for transfers between devices: 136 us -> none  [the longest x4 71.7 us: with_halo(): before = lax.ppermute(last, axis, up)]
    all_gather x1 -> x0, blocking collectives: 83.6 us -> none  [local(): slab_piece = lax.all_gather(coarse, 'tile', axis=1, tiled=True)]
    dot_general x47 -> x0, matrix products: 73.2 us -> none  [the longest x3 22.5 us: columns_transform(): jnp.dot(flattened, lookup, precision=PRECISE, preferred_element_type=jnp....]
    pallas_call x0 -> x1, Pallas kernels: none -> 63.8 us  [local_program(): pl.pallas_call(kernel, out_shape=jax.ShapeDtypeStruct((C, TX, TY), BF16),...]
    ppermute x8 -> x0, starting transfers between devices: 36.5 us -> none  [the longest x4 29.4 us: with_halo(): before = lax.ppermute(last, axis, up)]
    unnamed x31 -> x36, local copies, waits for them, and re-layouts: 0.34 us -> 17 us
    psum x1 -> x0, blocking collectives: 13.8 us -> none  [local(): coeffs = lax.psum(partial_sum, 'grp')]
    all_gather x1 -> x0, local copies, waits for them, and re-layouts: 7.39 us -> none  [local(): slab_piece = lax.all_gather(coarse, 'tile', axis=1, tiled=True)]
  transfers between devices with their start and end apart: 8 -> 0, of which waited for: 8 -> 0; matrix products, arithmetic and copies ran while one was open for 0% -> 0% of each run, Pallas kernels for 0% -> 0%
where the time goes in v1:
time: 81.6 us; the launch traced here: 80.8 us
  Pallas kernels  63.8 us (78%)
  local copies, waits for them, and re-layouts  17 us (21%)
    pallas_call x1, Pallas kernels, local_program(): pl.pallas_call(kernel, out_shape=jax.ShapeDtypeStruct((C, TX, TY), BF16),...  63.8 us
    unnamed x36, local copies, waits for them, and re-layouts  17 us

profile of v1, /device:TPU:1, one launch (start us, length us, event | category | flops | bytes accessed | tf_op | source)
XLA Modules:
  0.0 80.8 jit_solution(2612544445638956246)
XLA Ops:
  0.0 0.9 %copy.20.win_ref = bf16[2,128,64]{2,1,0:T(8,128)(2,1)S(1)} copy(bf16[2,128,64]{1,2,0:T(8,128)(2,1)} %param.24) | data formatting | bytes 65536 | tf_op args[5]
  0.9 0.0 copy-start
  0.9 1.6 %copy-done = f32[2,32,64,64]{3,2,1,0:T(8,128)S(1)} copy-done((f32[2,32,64,64]{3,2,1,0:T(8,128)S(1)}, f32[2,32,64,64]{3,2,1,0:T(8,128)}, u32[]{:S(2)}) %copy-start) | copy-done | bytes 1048600
  2.5 0.0 copy-start.1
  2.5 1.2 %copy-done.1 = bf16[64,64,128]{2,1,0:T(8,128)(2,1)S(1)} copy-done((bf16[64,64,128]{2,1,0:T(8,128)(2,1)S(1)}, bf16[64,64,128]{2,1,0:T(8,128)(2,1)}, u32[]{:S(2)}) %copy-start.1) | copy-done | bytes 1048600
  3.7 0.0 copy-start.2
  3.7 0.9 %copy-done.2 = f32[256,2,128]{2,1,0:T(2,128)S(1)} copy-done((f32[256,2,128]{2,1,0:T(2,128)S(1)}, f32[256,2,128]{2,1,0:T(2,128)}, u32[]{:S(2)}) %copy-start.2) | copy-done | bytes 262168
  4.6 0.0 copy-start.3
  4.7 0.9 %copy-done.3 = f32[128,512]{1,0:T(8,128)S(1)} copy-done((f32[128,512]{1,0:T(8,128)S(1)}, f32[128,512]{1,0:T(8,128)}, u32[]{:S(2)}) %copy-start.3) | copy-done | bytes 262168
  5.6 0.0 copy-start.4
  5.6 0.9 %copy-done.4 = f32[128,512]{1,0:T(8,128)S(1)} copy-done((f32[128,512]{1,0:T(8,128)S(1)}, f32[128,512]{1,0:T(8,128)}, u32[]{:S(2)}) %copy-start.4) | copy-done | bytes 262168
  6.5 0.0 copy-start.5
  6.6 0.9 %copy-done.5 = bf16[1024,128]{1,0:T(8,128)(2,1)S(1)} copy-done((bf16[1024,128]{1,0:T(8,128)(2,1)S(1)}, bf16[1024,128]{1,0:T(8,128)(2,1)}, u32[]{:S(2)}) %copy-start.5) | copy-done | bytes 262168
  7.5 0.0 copy-start.6
  7.5 0.9 %copy-done.6 = bf16[1024,128]{1,0:T(8,128)(2,1)S(1)} copy-done((bf16[1024,128]{1,0:T(8,128)(2,1)S(1)}, bf16[1024,128]{1,0:T(8,128)(2,1)}, u32[]{:S(2)}) %copy-start.6) | copy-done | bytes 262168
  8.4 0.0 copy-start.7
  8.5 0.9 %copy-done.7 = bf16[64,1024]{1,0:T(8,128)(2,1)S(1)} copy-done((bf16[64,1024]{1,0:T(8,128)(2,1)S(1)}, bf16[64,1024]{1,0:T(8,128)(2,1)}, u32[]{:S(2)}) %copy-start.7) | copy-done | bytes 131096
  9.4 0.0 copy-start.8
  9.4 0.8 %copy-done.8 = f32[128,128]{1,0:T(8,128)S(1)} copy-done((f32[128,128]{1,0:T(8,128)S(1)}, f32[128,128]{1,0:T(8,128)}, u32[]{:S(2)}) %copy-start.8) | copy-done | bytes 65560
  10.2 0.0 copy-start.9
  10.2 0.8 copy-done.9
  11.0 0.0 copy-start.10
  11.0 0.8 copy-done.10
  11.7 0.0 copy-start.11
  11.7 0.8 copy-done.11
  12.5 0.0 copy-start.12
  12.5 0.8 copy-done.12
  13.2 0.0 copy-start.13
  13.2 0.7 copy-done.13
  14.0 0.0 copy-start.14
  14.0 0.7 copy-done.14
  14.7 0.0 copy-start.15
  14.7 0.7 copy-done.15
  15.4 0.0 copy-start.16
  15.4 0.7 copy-done.16
  16.0 63.8 %ocean.1 = bf16[64,64,128]{2,1,0:T(8,128)(2,1)S(1)} custom-call(bf16[64,64,128]{2,1,0:T(8,128)(2,1)S(1)} %copy-done.1, s32[64,128]{1,0:T(8,128)S(1)} %copy-done.9, f32[2,2,2048,64]{3,2,1,0:T(8,128)} %bitcast.5, bf16[2,64,64]{2,1,0:T(8,128)(2,1)S(1)} %copy-done.10, f32[2,64]{1,0:T(2,128)S(1)} %copy-done.15, bf16[2,128,64]{2,1,0:T(8,128)(2,1)S(1)} %copy.20.win_ref, ...), custom_call_target="tpu_custom_call" | custom-call | tf_op jit(solution)/shard_map/ocean/pallas_call | solution.py:333
  79.8 1.0 %copy.22 = bf16[64,64,128]{2,1,0:T(8,128)(2,1)} copy(bf16[64,64,128]{2,1,0:T(8,128)(2,1)S(1)} %ocean.1) | data formatting | bytes 2097152
Async XLA Ops:
  0.9 1.6 %copy-start = (f32[2,32,64,64]{3,2,1,0:T(8,128)S(1)}, f32[2,32,64,64]{3,2,1,0:T(8,128)}, u32[]{:S(2)}) copy-start(f32[2,32,64,64]{3,2,1,0:T(8,128)} %param.26) | copy-start | bytes 3145732
  2.5 1.2 %copy-start.1 = (bf16[64,64,128]{2,1,0:T(8,128)(2,1)S(1)}, bf16[64,64,128]{2,1,0:T(8,128)(2,1)}, u32[]{:S(2)}) copy-start(bf16[64,64,128]{2,1,0:T(8,128)(2,1)} %x_ref.1) | copy-start | bytes 3145732
  3.7 0.9 %copy-start.2 = (f32[256,2,128]{2,1,0:T(2,128)S(1)}, f32[256,2,128]{2,1,0:T(2,128)}, u32[]{:S(2)}) copy-start(f32[256,2,128]{2,1,0:T(2,128)} %constant.26.clone.dev_ref) | copy-start | bytes 786436
  4.6 0.9 %copy-start.3 = (f32[128,512]{1,0:T(8,128)S(1)}, f32[128,512]{1,0:T(8,128)}, u32[]{:S(2)}) copy-start(f32[128,512]{1,0:T(8,128)} %constant.24.clone.spread) | copy-start | bytes 786436
  5.6 0.9 %copy-start.4 = (f32[128,512]{1,0:T(8,128)S(1)}, f32[128,512]{1,0:T(8,128)}, u32[]{:S(2)}) copy-start(f32[128,512]{1,0:T(8,128)} %constant.23.clone.stab) | copy-start | bytes 786436
  6.5 0.9 %copy-start.5 = (bf16[1024,128]{1,0:T(8,128)(2,1)S(1)}, bf16[1024,128]{1,0:T(8,128)(2,1)}, u32[]{:S(2)}) copy-start(bf16[1024,128]{1,0:T(8,128)(2,1)} %constant.20.clone.pool) | copy-start | bytes 786436
  7.5 0.9 %copy-start.6 = (bf16[1024,128]{1,0:T(8,128)(2,1)S(1)}, bf16[1024,128]{1,0:T(8,128)(2,1)}, u32[]{:S(2)}) copy-start(bf16[1024,128]{1,0:T(8,128)(2,1)} %constant.18.clone.table) | copy-start | bytes 786436
  8.4 0.9 %copy-start.7 = (bf16[64,1024]{1,0:T(8,128)(2,1)S(1)}, bf16[64,1024]{1,0:T(8,128)(2,1)}, u32[]{:S(2)}) copy-start(bf16[64,1024]{1,0:T(8,128)(2,1)} %constant.19.clone.basis) | copy-start | bytes 393220
  9.4 0.8 %copy-start.8 = (f32[128,128]{1,0:T(8,128)S(1)}, f32[128,128]{1,0:T(8,128)}, u32[]{:S(2)}) copy-start(f32[128,128]{1,0:T(8,128)} %constant.22.clone.ctab) | copy-start | bytes 196612
  10.2 0.8 copy-start.9
  11.0 0.8 copy-start.10
  11.7 0.8 copy-start.11
  12.5 0.8 copy-start.12
  13.2 0.7 copy-start.13
  14.0 0.7 copy-start.14
  14.7 0.7 copy-start.15
  15.4 0.7 copy-start.16

commit v2 on v1

v2 whole, which is shorter than its diff:
```python
import functools
import math

import jax
import jax.numpy as jnp
import numpy as np
from jax import lax
from jax.experimental import pallas as pl
from jax.experimental.pallas import tpu as pltpu
from jax.sharding import PartitionSpec as P

MESH = pl.DeviceIdType.MESH
F32 = jnp.float32
BF16 = jnp.bfloat16
PRECISE = lax.Precision.HIGHEST

C = 64
F = 128
TX = 64
TY = 128
L1 = 192
L2 = 256
NT = 64
NG = 4
PAD = 72
GROUPS = 8
GELU0 = math.sqrt(2.0 / math.pi)
GELU1 = GELU0 * 0.044715


def lane_numbers():
    lane = np.arange(128)
    ri, half, k = lane // 64, (lane // 32) % 2, lane % 32
    i, j = k // 4, k % 4
    kappa = np.where(i < 4, i, i - 8)
    return ri, half, kappa, j


def constants():
    ri, half, kappa, j = lane_numbers()
    two_pi = 2.0 * np.pi
    cell = np.arange(1024)
    b, q = cell // 128, cell % 128

    phi = two_pi * (b[:, None] * kappa / L1 + (q % 64)[:, None] * j / L2)
    table = np.where(ri == 0, np.cos(phi), -np.sin(phi)) * ((q // 64)[:, None] == half)

    rows = np.arange(64)
    ri_r, k_r = rows // 32, rows % 32
    i_r, j_r = k_r // 4, k_r % 4
    kap_r = np.where(i_r < 4, i_r, i_r - 8)
    phi = two_pi * (kap_r[:, None] * (64 + b) / L1 + j_r[:, None] * (64 + q) / L2)
    basis = np.where(ri_r[:, None] == 0, np.cos(phi), -np.sin(phi))

    pool = ((np.arange(128) % 8)[None, :] == (q // 16)[:, None]) & (np.arange(128) < 32)[None, :]

    def forward(theta):
        return np.cos(theta), np.where(ri == 0, 1.0, -1.0) * np.sin(theta)

    weight = np.where(j == 0, 1.0, 2.0)
    rot = []
    for a in range(GROUPS):
        rot += list(forward(two_pi * kappa * a / 24))
    for rho in range(3):
        rot += list(forward(two_pi * kappa * rho / 3))
    rot += list(forward(two_pi * j * np.where(half == 0, 1, 2) / 4))
    rot += list(forward(two_pi * j * 3 / 4))
    for a in range(GROUPS):
        cos, sin = forward(two_pi * kappa * a / 24)
        rot += [0.5 * cos * weight / (L1 * L2), -0.5 * sin * weight / (L1 * L2)]
    rot = np.stack(rot)
    rot = np.concatenate([rot, np.zeros((48 - rot.shape[0], 128))])

    small = np.arange(128)
    br, bq = small // 8, small % 8
    theta = two_pi * (br[:, None] * kappa / 256 + bq[:, None] * j / 32)
    ctab = np.where(ri == 0, np.cos(theta), -np.sin(theta)) * (small < 32)[:, None]
    wide = np.arange(512)
    wr, wq = wide // 128, (wide % 128) // 16
    theta = two_pi * (kappa[:, None] * wr / 256 + j[:, None] * wq / 32)
    stab = np.where(ri[:, None] == 0, np.cos(theta), -np.sin(theta)) * weight[:, None] / (256 * 32)
    stab = stab * (half == 0)[:, None]
    spread = ((br[:, None] == wr) & (bq[:, None] == wq) & (small < 32)[:, None])

    place = np.zeros((64, 128))
    for c in range(64):
        place[c, (32 + c) if c < 32 else (64 + c)] = 1.0

    dev = np.zeros((NT * NG, 2, 128))
    for t in range(NT):
        for g in range(NG):
            dev[t * NG + g, 0], dev[t * NG + g, 1] = forward(two_pi * ((kappa * t % 64) / 64 + (j * g % 4) / 4))
    late = np.concatenate([ctab, stab, spread], axis=1)
    return dict(
        table=table.astype(BF16),
        basis=basis.astype(BF16),
        pool=pool.astype(np.float32).astype(BF16),
        place=place.astype(BF16),
        rot=rot.astype(np.float32),
        late=late.astype(np.float32),
        dev=dev.astype(np.float32),
    )


ROW3, OWN, REC, SYN = 16, 22, 24, 26


def gelu_of_double(h):
    return h + h * jnp.tanh(h * (2.0 * GELU0 + 8.0 * GELU1 * (h * h)))


def dot(a, b):
    return jnp.dot(a, b, preferred_element_type=F32)


def exact(a, b):
    return jnp.dot(a, b, precision=PRECISE, preferred_element_type=F32)


XCHUNKS = 4
UNROLL = 3


def kernel(
    x_hbm, mask_hbm, w_hbm, wp_hbm, bp_hbm, win_hbm, wout_hbm, wc_hbm, cp_hbm, cb_hbm,
    table_hbm, basis_hbm, pool_hbm, place_hbm, rot_hbm, late_hbm, dev_hbm,
    out_ref,
    x_ref, mask_ref, wv, wp_ref, bp_ref, wint_ref, wout_ref, cp_ref, cb_ref,
    table, basis, pool, place, rot, late, devv,
    xs, mf, fa, fb, wb, lhs, wpad, win, bias, pre_s, hid_s, esend, erecv, csend, crecv, local, cx,
    lsem, ssem, rsem,
):
    t = lax.axis_index("tile")
    g = lax.axis_index("grp")

    count = [0]

    def load(src, dst):
        copy = pltpu.make_async_copy(src, dst, lsem.at[count[0]])
        count[0] += 1
        copy.start()
        return copy

    step_c = C // XCHUNKS
    get_mask = load(mask_hbm, mask_ref)
    get_x = [load(x_hbm.at[pl.ds(n * step_c, step_c)], x_ref.at[pl.ds(n * step_c, step_c)]) for n in range(XCHUNKS)]
    get_table = load(table_hbm, table)
    get_rot = load(rot_hbm, rot)
    get_w = [load(w_hbm.at[0], wv.at[0])]
    get_small = [
        load(wp_hbm, wp_ref), load(bp_hbm, bp_ref), load(win_hbm, wint_ref), load(wout_hbm, wout_ref),
        load(cp_hbm, cp_ref), load(cb_hbm, cb_ref), load(place_hbm, place), load(basis_hbm, basis),
    ]
    get_w.append(load(w_hbm.at[1], wv.at[1]))
    get_w.append(load(wc_hbm, wv.at[2]))
    get_late = [load(pool_hbm, pool), load(late_hbm, late), load(dev_hbm.at[t * NG + g], devv)]

    def at(tile, grp):
        return {"tile": tile, "grp": grp}

    around = []
    for dt in (-1, 0, 1):
        for dg in (-1, 0, 1):
            if dt or dg:
                around.append((dt, dg, at(lax.rem(t + (dt + NT), NT), lax.rem(g + (dg + NG), NG))))
    yc, xc, zlo = lax.rem(t, 8), lax.div(t, 16), lax.rem(lax.div(t, 8), 2)
    zc = 2 * g + zlo
    plane = []
    for dx in range(4):
        row = lax.rem(xc + dx, 4) * 16 + zlo * 8
        plane += [at(row + lax.rem(yc + d, 8), g) for d in range(8) if dx or d]
    along_z = []
    for d in range(1, 8):
        z = lax.rem(zc + d, 8)
        along_z.append(at(xc * 16 + lax.rem(z, 2) * 8 + yc, lax.div(z, 2)))

    barrier = pltpu.get_barrier_semaphore()
    partners = [device for _, _, device in around] + plane + along_z
    for partner in partners:
        pl.semaphore_signal(barrier, inc=1, device_id=partner, device_id_type=MESH)

    lane = lax.broadcasted_iota(jnp.int32, (64, 128), 1)
    mode = lane % 32
    in_a = (lane // 32) % 2 == 0
    in_a32 = in_a[:32]
    re_sign = jnp.where(lane < 64, -1.0, 1.0).astype(F32)

    def turned(v, row):
        return v * rot[row : row + 1, :] + pltpu.roll(v, 64, 1) * rot[row + 1 : row + 2, :]

    get_mask.wait()
    mf[...] = mask_ref[...].astype(F32)

    def mask_step(c, carry):
        xs[pl.ds(pl.multiple_of(c * PAD, 8), 64), :] = jnp.where(mask_ref[...] > 0, x_ref[c].astype(F32), 0.0)
        return carry

    for n in range(XCHUNKS):
        get_x[n].wait()
        lax.fori_loop(n * step_c, (n + 1) * step_c, mask_step, 0, unroll=4)

    def group_step(a, carry):
        for b in range(8):
            fa[a + 1, :, b * 128 : (b + 1) * 128] = xs[pl.ds(8 * a + b, 64, stride=PAD), :].astype(BF16)
        return carry

    lax.fori_loop(0, GROUPS, group_step, 0)

    get_table.wait()
    get_rot.wait()
    parts = dot(fa[1:].reshape(512, 1024), table[...])
    total = turned(parts[:64], 0)
    for a in range(1, GROUPS):
        total = total + turned(parts[a * 64 : (a + 1) * 64], 2 * a)

    def remote(src, dst, number, device):
        return pltpu.make_async_remote_copy(
            src_ref=src, dst_ref=dst, send_sem=ssem.at[number], recv_sem=rsem.at[number],
            device_id=device, device_id_type=MESH,
        )

    def prepare(l):
        get_w[l].wait()

        def prepare_step(n, carry):
            rows = pl.ds(pl.multiple_of(n * 256, 256), 256)
            late_rows = pl.ds(pl.multiple_of(1024 + n * 256, 256), 256)
            wb[l, rows, :128] = jnp.concatenate([wv[l, 0, rows, :], wv[l, 1, rows, :]], axis=1).astype(BF16)
            wb[l, rows, 128:] = jnp.concatenate([wv[l, 0, late_rows, :], wv[l, 1, late_rows, :]], axis=1).astype(BF16)
            return carry

        lax.fori_loop(0, 4, prepare_step, 0)

    def exchange(l, total, beside):
        whole = turned(total, OWN)
        whole = whole + pltpu.roll(whole, 96, 1)
        packed = jnp.where(in_a32, whole[:32], pltpu.roll(whole[32:], 32, 1))
        esend[l, 1] = packed.astype(BF16)
        esend[l, 0] = jnp.where(in_a32, total[:32], pltpu.roll(total[32:], 32, 1)).astype(BF16)
        esend[l, 2] = jnp.where(in_a32, pltpu.roll(total[:32], 96, 1), total[32:]).astype(BF16)
        sends = []
        for n, (dt, dg, device) in enumerate(around):
            sends.append(remote(esend.at[l, dg + 1], erecv.at[l, 1 - dt, 1 - dg], 8 * l + n, device))
        for s in sends:
            s.start()
        beside()
        for s in sends:
            s.wait()
        rows = (t > 0, None, t < NT - 1)
        total = None
        for r in range(3):
            from_left = jnp.where(g > 0, erecv[l, r, 0].astype(F32), 0.0)
            from_right = jnp.where(g < NG - 1, erecv[l, r, 2].astype(F32), 0.0)
            middle = packed if r == 1 else erecv[l, r, 1].astype(F32)
            one = turned(middle + from_left + turned(from_right, REC), ROW3 + 2 * r)
            if rows[r] is not None:
                one = jnp.where(rows[r], one, 0.0)
            total = one if total is None else total + one
        return jnp.concatenate([total, pltpu.roll(total, 96, 1)], axis=0)

    def mix(l, u):
        sides = jnp.concatenate([u, pltpu.roll(u, 64, 1) * re_sign], axis=0).astype(BF16)
        none = jnp.zeros_like(sides)
        both = jnp.concatenate(
            [jnp.concatenate([sides, none], axis=1), jnp.concatenate([none, sides], axis=1)], axis=0
        )
        acc = jnp.zeros((64, 128), F32)
        for block in range(4):
            o = dot(wb[l, block * 256 : (block + 1) * 256, :], both)
            for n in range(4):
                k = block * 4 + n
                acc = jnp.where(mode == k, o[n * 64 : (n + 1) * 64, :128], acc)
                acc = jnp.where(mode == k + 16, o[n * 64 : (n + 1) * 64, 128:], acc)
        return acc

    def layer(l, src, dst, v, matrix, finish):
        swapped = pltpu.roll(v, 64, 1)
        for a in range(GROUPS):
            lhs[a] = jnp.where(in_a, v * rot[SYN + 2 * a : SYN + 2 * a + 1, :] + swapped * rot[SYN + 2 * a + 1 : SYN + 2 * a + 2, :], wpad[l]).astype(BF16)
        shift = jnp.concatenate([bias[l], bias[l]], axis=1)

        def first(a, cols):
            rhs = jnp.concatenate(
                [basis[:32, cols], src[a + 1, :32, cols], basis[32:, cols], src[a + 1, 32:, cols]], axis=0
            )
            return dot(lhs[a], rhs)

        def second(pre):
            return dot(win[l], gelu_of_double(pre + shift).astype(BF16))

        def third(hid, row):
            sea = jnp.concatenate([mf[pl.ds(row, 1), :], mf[pl.ds(row + 1, 1), :]], axis=1)
            return (dot(wout_ref[l], gelu_of_double(hid).astype(BF16)) * sea).astype(BF16)

        def step(i, total):
            for inner in range(UNROLL):
                a = UNROLL * i + inner
                part = None
                for n in range(4):
                    m = (n + 2) % 4
                    cols = slice(n * 256, (n + 1) * 256)
                    pre_s[n] = first(jnp.minimum(a, GROUPS - 1), cols)
                    hid_s[m] = second(pre_s[m])
                    new = third(hid_s[n], jnp.maximum(8 * a - 8 + 2 * n, 0))
                    dst[a, :, cols] = new
                    piece = dot(new, matrix[cols, :])
                    part = piece if n == 0 else part + piece
                total = finish(a - 1, part, total)
            return total

        return lax.fori_loop(0, (GROUPS + 1) // UNROLL, step, jnp.zeros((64, 128), F32))

    def analysis(a, part, total):
        at_a = 2 * jnp.maximum(a, 0)
        part = part * rot[pl.ds(at_a, 1), :] + pltpu.roll(part, 64, 1) * rot[pl.ds(at_a + 1, 1), :]
        return total + jnp.where(a >= 0, part, 0.0)

    for copy in get_small:
        copy.wait()
    eye = lax.broadcasted_iota(jnp.int32, (64, 64), 0) == lax.broadcasted_iota(jnp.int32, (64, 64), 1)

    def column(row):
        return jnp.broadcast_to(jnp.sum(jnp.where(eye, row, 0.0), axis=1, keepdims=True), (64, 128))

    for l in range(2):
        wpad[l] = 0.5 * dot(wp_ref[l], place[...])
        win[l] = (0.5 * wint_ref[l].astype(F32)).T.astype(BF16)
        bias[l] = 0.5 * column(bp_ref[l : l + 1, :])
    bias[2] = column(cb_ref[...])

    pl.semaphore_wait(barrier, len(partners))
    u = exchange(0, total, lambda: prepare(0))
    v = mix(0, u)
    total = layer(0, fa, fb, v, table, analysis)
    u = exchange(1, total, lambda: prepare(1))
    v = mix(1, u)
    for copy in get_late:
        copy.wait()

    def pooled(a, part, total):
        return total + jnp.where((lane // 8 == a // 2) & (a >= 0), part, 0.0)

    coarse = layer(1, fb, fa, v, pool, pooled) * (1.0 / 256.0)

    cos, sin = devv[0:1, :], devv[1:2, :]
    part = exact(coarse, late[:, :128])
    part = part * cos + pltpu.roll(part, 64, 1) * sin
    acc = jnp.where(in_a32, part[:32], part[32:])
    number, slot = 16, 0
    for stage, peers in enumerate((plane, along_z)):
        csend[stage] = acc.astype(BF16)
        sends = []
        for peer in peers:
            sends.append(remote(csend.at[stage], crecv.at[slot], number, peer))
            number, slot = number + 1, slot + 1
        for s in sends:
            s.start()
        if stage == 0:
            local[...] = exact(cp_ref[...], exact(coarse, late[:, 640:])) + jnp.concatenate([bias[2]] * 4, axis=1)
            prepare(2)
        else:
            def back_step(a, carry):
                for b in range(8):
                    xs[pl.ds(8 * a + b, 64, stride=PAD), :] = fa[a + 1, :, b * 128 : (b + 1) * 128].astype(F32)
                return carry

            lax.fori_loop(0, GROUPS, back_step, 0)
        for s in sends:
            s.wait()
        for n in range(slot - len(peers), slot):
            acc = acc + crecv[n].astype(F32)
    u = jnp.concatenate([acc, pltpu.roll(acc, 96, 1)], axis=0)
    v = mix(2, u)
    v = v * cos - pltpu.roll(v, 64, 1) * sin
    full = exact(jnp.where(in_a, v, 0.0), late[:, 128:640]) + local[...]
    for n in range(4):
        cx[n] = full[:, n * 128 : (n + 1) * 128]

    def final_step(c, carry):
        rows = []
        for n in range(4):
            fix = jnp.broadcast_to(cx[n, pl.ds(c, 1), :], (16, 128))
            base = pl.multiple_of(c * PAD, 8)
            rows.append(xs[pl.ds(base + 16 * n, 16), :] + fix * mf[16 * n : 16 * (n + 1), :])
        out_ref[c] = jnp.concatenate(rows, axis=0).astype(BF16)
        return carry

    lax.fori_loop(0, C, final_step, 0, unroll=4)


def local_program(consts, x, mask, w, wp, bp, win, wout, wc, cp, cb):
    hbm = pl.BlockSpec(memory_space=pltpu.HBM)
    n_remote = 16 + 38
    names = ["table", "basis", "pool", "place", "rot", "late", "dev"]
    return pl.pallas_call(
        kernel,
        out_shape=jax.ShapeDtypeStruct((C, TX, TY), BF16),
        in_specs=[hbm] * (10 + len(names)),
        out_specs=pl.BlockSpec(memory_space=pltpu.VMEM),
        scratch_shapes=[
            pltpu.VMEM((C, TX, TY), BF16),
            pltpu.VMEM((TX, TY), jnp.int32),
            pltpu.VMEM((3, 2, 2048, 64), F32),
            pltpu.VMEM((2, C, C), BF16),
            pltpu.VMEM((2, C), F32),
            pltpu.VMEM((2, C, F), BF16),
            pltpu.VMEM((2, C, F), BF16),
            pltpu.VMEM((C, C), F32),
            pltpu.VMEM((1, C), F32),
            pltpu.VMEM((1024, 128), BF16),
            pltpu.VMEM((64, 1024), BF16),
            pltpu.VMEM((1024, 128), BF16),
            pltpu.VMEM((64, 128), BF16),
            pltpu.VMEM((48, 128), F32),
            pltpu.VMEM((128, 1152), F32),
            pltpu.VMEM((2, 128), F32),
            pltpu.VMEM((C * PAD, 128), F32),
            pltpu.VMEM((TX, TY), F32),
            pltpu.VMEM((GROUPS + 1, C, 1024), BF16),
            pltpu.VMEM((GROUPS + 1, C, 1024), BF16),
            pltpu.VMEM((3, 1024, 256), BF16),
            pltpu.VMEM((GROUPS, C, 128), BF16),
            pltpu.VMEM((2, C, 128), F32),
            pltpu.VMEM((2, F, C), BF16),
            pltpu.VMEM((3, C, 128), F32),
            pltpu.VMEM((4, C, 256), F32),
            pltpu.VMEM((4, F, 256), F32),
            pltpu.VMEM((2, 3, 32, 128), BF16),
            pltpu.VMEM((2, 3, 3, 32, 128), BF16),
            pltpu.VMEM((2, 32, 128), BF16),
            pltpu.VMEM((38, 32, 128), BF16),
            pltpu.VMEM((C, 512), F32),
            pltpu.VMEM((4, C, 128), F32),
            pltpu.SemaphoreType.DMA((22,)),
            pltpu.SemaphoreType.DMA((n_remote,)),
            pltpu.SemaphoreType.DMA((n_remote,)),
        ],
        compiler_params=pltpu.CompilerParams(
            collective_id=0, has_side_effects=True, vmem_limit_bytes=48000 * 1024
        ),
        name="ocean",
    )(
        *[
            pltpu.with_memory_space_constraint(v, pltpu.HBM)
            for v in (
                x, mask, w.reshape(2, 2, 2048, 64), wp, bp, jnp.swapaxes(win, 1, 2), wout,
                wc.reshape(2, 2048, 64), cp, cb.reshape(1, 64), *[consts[name] for name in names],
            )
        ]
    )


def solution(mesh):
    consts = constants()

    def body(*args):
        return local_program({k: jnp.asarray(v) for k, v in consts.items()}, *args)

    placed = (P(None, "tile", "grp"), P("tile", "grp"), P(), P(), P(), P(), P(), P(), P(), P())
    return jax.shard_map(body, mesh=mesh, in_specs=placed, out_specs=P(None, "tile", "grp"), check_vma=False)
```

time: 81.6 us -> 45.5 us (0.56)
  Pallas kernels: 63.8 us -> 44.4 us
  local copies, waits for them, and re-layouts: 17 us -> 0.97 us
    pallas_call x1, Pallas kernels: 63.8 us -> 44.4 us  [local_program(): pl.pallas_call(kernel, out_shape=jax.ShapeDtypeStruct((C, TX, TY), BF16),...]
    unnamed x36 -> x1, local copies, waits for them, and re-layouts: 17 us -> 0.97 us
where the time goes in v2:
time: 45.5 us; the launch traced here: 45.4 us
  Pallas kernels  44.4 us (98%)
  local copies, waits for them, and re-layouts  0.97 us (2%)
    pallas_call x1, Pallas kernels, local_program(): pl.pallas_call(kernel, out_shape=jax.ShapeDtypeStruct((C, TX, TY), BF16),...  44.4 us
    unnamed x1, local copies, waits for them, and re-layouts  0.97 us

profile of v2, /device:TPU:1, one launch (start us, length us, event | category | flops | bytes accessed | tf_op | source)
XLA Modules:
  0.0 45.4 jit_solution(8146309152198717548)
XLA Ops:
  0.0 44.4 %ocean.1 = bf16[64,64,128]{2,1,0:T(8,128)(2,1)S(1)} custom-call(bf16[64,64,128]{2,1,0:T(8,128)(2,1)} %x_hbm.1, s32[64,128]{1,0:T(8,128)} %mask_hbm.1, f32[2,2,2048,64]{3,2,1,0:T(8,128)} %bitcast.4, bf16[2,64,64]{2,1,0:T(8,128)(2,1)} %wp_hbm.1, f32[2,64]{1,0:T(2,128)} %bp_hbm.1, bf16[2,64,128]{2,1,0:T(8,128)(2,1)} %bitcast.6, bf16[2,64,128]{2,1,0:T(8,128)(2,1)} %wout_hbm.1, ...), custom_call_target="tpu_custom_call" | custom-call | tf_op jit(solution)/shard_map/ocean/pallas_call | solution.py:395
  44.4 1.0 %copy.19 = bf16[64,64,128]{2,1,0:T(8,128)(2,1)} copy(bf16[64,64,128]{2,1,0:T(8,128)(2,1)S(1)} %ocean.1) | data formatting | bytes 2097152

commit v3 on v2

--- a/solution.py
+++ b/solution.py
@@ -51,6 +51,8 @@
     kap_r = np.where(i_r < 4, i_r, i_r - 8)
     phi = two_pi * (kap_r[:, None] * (64 + b) / L1 + j_r[:, None] * (64 + q) / L2)
     basis = np.where(ri_r[:, None] == 0, np.cos(phi), -np.sin(phi))
+    basis[32] = 1.0
+    basis = basis.reshape(64, 8, 128).transpose(1, 0, 2)
 
     pool = ((np.arange(128) % 8)[None, :] == (q // 16)[:, None]) & (np.arange(128) < 32)[None, :]
 
@@ -67,7 +69,8 @@
     rot += list(forward(two_pi * j * 3 / 4))
     for a in range(GROUPS):
         cos, sin = forward(two_pi * kappa * a / 24)
-        rot += [0.5 * cos * weight / (L1 * L2), -0.5 * sin * weight / (L1 * L2)]
+        keep = 0.5 * weight / (L1 * L2) * (half == 0) * (np.arange(128) != 64)
+        rot += [keep * cos, -keep * sin]
     rot = np.stack(rot)
     rot = np.concatenate([rot, np.zeros((48 - rot.shape[0], 128))])
 
@@ -90,14 +93,17 @@
     for t in range(NT):
         for g in range(NG):
             dev[t * NG + g, 0], dev[t * NG + g, 1] = forward(two_pi * ((kappa * t % 64) / 64 + (j * g % 4) / 4))
-    late = np.concatenate([ctab, stab, spread], axis=1)
+    high = ctab.astype(np.float32).astype(BF16).astype(np.float64)
+    ctab3 = np.concatenate([high[:32], high[:32], (ctab - high)[:32], np.zeros((32, 128))])
+    sums = np.concatenate([np.concatenate([stab] * 2, axis=0), np.concatenate([ctab3, np.zeros((128, 128))])], axis=1)
     return dict(
         table=table.astype(BF16),
         basis=basis.astype(BF16),
         pool=pool.astype(np.float32).astype(BF16),
         place=place.astype(BF16),
         rot=rot.astype(np.float32),
-        late=late.astype(np.float32),
+        sums=sums.astype(np.float32).astype(BF16),
+        late=spread.astype(np.float32),
         dev=dev.astype(np.float32),
     )
 
@@ -118,16 +124,16 @@
 
 
 XCHUNKS = 4
-UNROLL = 3
+UNROLL = 9
 
 
 def kernel(
     x_hbm, mask_hbm, w_hbm, wp_hbm, bp_hbm, win_hbm, wout_hbm, wc_hbm, cp_hbm, cb_hbm,
-    table_hbm, basis_hbm, pool_hbm, place_hbm, rot_hbm, late_hbm, dev_hbm,
+    table_hbm, basis_hbm, pool_hbm, place_hbm, rot_hbm, sums_hbm, late_hbm, dev_hbm,
     out_ref,
     x_ref, mask_ref, wv, wp_ref, bp_ref, wint_ref, wout_ref, cp_ref, cb_ref,
-    table, basis, pool, place, rot, late, devv,
-    xs, mf, fa, fb, wb, lhs, wpad, win, bias, pre_s, hid_s, esend, erecv, csend, crecv, local, cx,
+    table, basis, pool, place, rot, sums, late, devv,
+    xs, mf, fa, fb, wb, lhs, wpad, win, bias, pre_s, hid_s, parts_s, esend, erecv, csend, crecv, local, cx,
     lsem, ssem, rsem,
 ):
     t = lax.axis_index("tile")
@@ -144,25 +150,20 @@
     step_c = C // XCHUNKS
     get_mask = load(mask_hbm, mask_ref)
     get_x = [load(x_hbm.at[pl.ds(n * step_c, step_c)], x_ref.at[pl.ds(n * step_c, step_c)]) for n in range(XCHUNKS)]
-    get_table = load(table_hbm, table)
-    get_rot = load(rot_hbm, rot)
-    get_w = [load(w_hbm.at[0], wv.at[0])]
-    get_small = [
-        load(wp_hbm, wp_ref), load(bp_hbm, bp_ref), load(win_hbm, wint_ref), load(wout_hbm, wout_ref),
-        load(cp_hbm, cp_ref), load(cb_hbm, cb_ref), load(place_hbm, place), load(basis_hbm, basis),
-    ]
-    get_w.append(load(w_hbm.at[1], wv.at[1]))
-    get_w.append(load(wc_hbm, wv.at[2]))
-    get_late = [load(pool_hbm, pool), load(late_hbm, late), load(dev_hbm.at[t * NG + g], devv)]
-
     def at(tile, grp):
         return {"tile": tile, "grp": grp}
 
+    row_there = {-1: t > 0, 1: t < NT - 1}
+    column_there = {-1: g > 0, 1: g < NG - 1}
+
+    def there(dt, dg):
+        if dt and dg:
+            return row_there[dt] & column_there[dg]
+        return row_there[dt] if dt else column_there[dg]
+
     around = []
-    for dt in (-1, 0, 1):
-        for dg in (-1, 0, 1):
-            if dt or dg:
-                around.append((dt, dg, at(lax.rem(t + (dt + NT), NT), lax.rem(g + (dg + NG), NG))))
+    for dt, dg in ((-1, -1), (-1, 1), (1, -1), (1, 1), (-1, 0), (1, 0), (0, -1), (0, 1)):
+        around.append((dt, dg, at(lax.rem(t + (dt + NT), NT), lax.rem(g + (dg + NG), NG))))
     yc, xc, zlo = lax.rem(t, 8), lax.div(t, 16), lax.rem(lax.div(t, 8), 2)
     zc = 2 * g + zlo
     plane = []
@@ -175,9 +176,27 @@
         along_z.append(at(xc * 16 + lax.rem(z, 2) * 8 + yc, lax.div(z, 2)))
 
     barrier = pltpu.get_barrier_semaphore()
-    partners = [device for _, _, device in around] + plane + along_z
-    for partner in partners:
+    expected = jnp.int32(len(plane) + len(along_z))
+    for dt, dg, device in around:
+        expected = expected + there(dt, dg).astype(jnp.int32)
+
+        @pl.when(there(dt, dg))
+        def greet(device=device):
+            pl.semaphore_signal(barrier, inc=1, device_id=device, device_id_type=MESH)
+
+    for partner in along_z + plane:
         pl.semaphore_signal(barrier, inc=1, device_id=partner, device_id_type=MESH)
+
+    get_table = load(table_hbm, table)
+    get_rot = load(rot_hbm, rot)
+    get_w = [load(w_hbm.at[0], wv.at[0])]
+    get_small = [
+        load(wp_hbm, wp_ref), load(bp_hbm, bp_ref), load(win_hbm, wint_ref), load(wout_hbm, wout_ref),
+        load(cp_hbm, cp_ref), load(cb_hbm, cb_ref), load(place_hbm, place), load(basis_hbm, basis),
+    ]
+    get_w.append(load(w_hbm.at[1], wv.at[1]))
+    get_w.append(load(wc_hbm, wv.at[2]))
+    get_late = [load(pool_hbm, pool), load(sums_hbm, sums), load(late_hbm, late), load(dev_hbm.at[t * NG + g], devv)]
 
     lane = lax.broadcasted_iota(jnp.int32, (64, 128), 1)
     mode = lane % 32
@@ -201,14 +220,14 @@
 
     def group_step(a, carry):
         for b in range(8):
-            fa[a + 1, :, b * 128 : (b + 1) * 128] = xs[pl.ds(8 * a + b, 64, stride=PAD), :].astype(BF16)
+            fa[a + 1, b] = xs[pl.ds(8 * a + b, 64, stride=PAD), :].astype(BF16)
         return carry
 
     lax.fori_loop(0, GROUPS, group_step, 0)
 
     get_table.wait()
     get_rot.wait()
-    parts = dot(fa[1:].reshape(512, 1024), table[...])
+    parts = dot(jnp.concatenate([fa[1:, b].reshape(512, 128) for b in range(8)], axis=1), table[...])
     total = turned(parts[:64], 0)
     for a in range(1, GROUPS):
         total = total + turned(parts[a * 64 : (a + 1) * 64], 2 * a)
@@ -241,11 +260,12 @@
         sends = []
         for n, (dt, dg, device) in enumerate(around):
             sends.append(remote(esend.at[l, dg + 1], erecv.at[l, 1 - dt, 1 - dg], 8 * l + n, device))
-        for s in sends:
-            s.start()
+        for (dt, dg, _), send in zip(around, sends):
+            pl.when(there(dt, dg))(send.start)
         beside()
-        for s in sends:
-            s.wait()
+        for (dt, dg, _), send in zip(around, sends):
+            pl.when(there(dt, dg))(send.wait_send)
+            pl.when(there(-dt, -dg))(send.wait_recv)
         rows = (t > 0, None, t < NT - 1)
         total = None
         for r in range(3):
@@ -275,45 +295,54 @@
 
     def layer(l, src, dst, v, matrix, finish):
         swapped = pltpu.roll(v, 64, 1)
+
+        def synthesis(a):
+            row = SYN + 2 * a
+            return v * rot[row : row + 1, :] + swapped * rot[row + 1 : row + 2, :]
+
+        fixed = wpad[l]
+        whole = synthesis(0) + fixed
+        rest = whole - whole.astype(BF16).astype(F32)
+        fixed = fixed + jnp.where(lane == 64, pltpu.roll(rest, 64, 1), 0.0)
         for a in range(GROUPS):
-            lhs[a] = jnp.where(in_a, v * rot[SYN + 2 * a : SYN + 2 * a + 1, :] + swapped * rot[SYN + 2 * a + 1 : SYN + 2 * a + 2, :], wpad[l]).astype(BF16)
-        shift = jnp.concatenate([bias[l], bias[l]], axis=1)
-
-        def first(a, cols):
-            rhs = jnp.concatenate(
-                [basis[:32, cols], src[a + 1, :32, cols], basis[32:, cols], src[a + 1, 32:, cols]], axis=0
-            )
-            return dot(lhs[a], rhs)
+            lhs[a] = (synthesis(a) + fixed).astype(BF16)
+
+        def first(a, n):
+            rhs = [
+                jnp.concatenate([basis[b, :32], src[a + 1, b, :32], basis[b, 32:], src[a + 1, b, 32:]], axis=0)
+                for b in (2 * n, 2 * n + 1)
+            ]
+            return dot(lhs[a], jnp.concatenate(rhs, axis=1))
 
         def second(pre):
-            return dot(win[l], gelu_of_double(pre + shift).astype(BF16))
+            return dot(win[l], gelu_of_double(pre).astype(BF16))
 
         def third(hid, row):
-            sea = jnp.concatenate([mf[pl.ds(row, 1), :], mf[pl.ds(row + 1, 1), :]], axis=1)
-            return (dot(wout_ref[l], gelu_of_double(hid).astype(BF16)) * sea).astype(BF16)
-
-        def step(i, total):
+            sea = [jnp.broadcast_to(mf[pl.ds(row + b, 1), :], (16, 128)).astype(BF16) for b in range(2)]
+            sea = jnp.concatenate([jnp.concatenate(sea, axis=1)] * 4, axis=0)
+            return dot(wout_ref[l], gelu_of_double(hid).astype(BF16)).astype(BF16) * sea
+
+        def step(i, carry):
             for inner in range(UNROLL):
                 a = UNROLL * i + inner
-                part = None
                 for n in range(4):
-                    m = (n + 2) % 4
-                    cols = slice(n * 256, (n + 1) * 256)
-                    pre_s[n] = first(jnp.minimum(a, GROUPS - 1), cols)
-                    hid_s[m] = second(pre_s[m])
+                    pre_s[n] = first(jnp.minimum(a, GROUPS - 1), n)
                     new = third(hid_s[n], jnp.maximum(8 * a - 8 + 2 * n, 0))
-                    dst[a, :, cols] = new
-                    piece = dot(new, matrix[cols, :])
-                    part = piece if n == 0 else part + piece
-                total = finish(a - 1, part, total)
-            return total
-
-        return lax.fori_loop(0, (GROUPS + 1) // UNROLL, step, jnp.zeros((64, 128), F32))
-
-    def analysis(a, part, total):
-        at_a = 2 * jnp.maximum(a, 0)
-        part = part * rot[pl.ds(at_a, 1), :] + pltpu.roll(part, 64, 1) * rot[pl.ds(at_a + 1, 1), :]
-        return total + jnp.where(a >= 0, part, 0.0)
+                    hid_s[(n + 2) % 4] = second(pre_s[(n + 2) % 4])
+                    dst[a, 2 * n] = new[:, :128]
+                    dst[a, 2 * n + 1] = new[:, 128:]
+                back = a
+                parts_s[back] = dot(jnp.concatenate([dst[back, b] for b in range(8)], axis=1), matrix[...])
+            return carry
+
+        lax.fori_loop(0, (GROUPS + 1) // UNROLL, step, 0)
+        return finish([parts_s[a + 1] for a in range(GROUPS)])
+
+    def analysis(parts):
+        total = turned(parts[0], 0)
+        for a in range(1, GROUPS):
+            total = total + turned(parts[a], 2 * a)
+        return total
 
     for copy in get_small:
         copy.wait()
@@ -323,12 +352,11 @@
         return jnp.broadcast_to(jnp.sum(jnp.where(eye, row, 0.0), axis=1, keepdims=True), (64, 128))
 
     for l in range(2):
-        wpad[l] = 0.5 * dot(wp_ref[l], place[...])
+        wpad[l] = 0.5 * dot(wp_ref[l], place[...]) + jnp.where(lane == 0, 0.5 * column(bp_ref[l : l + 1, :]), 0.0)
         win[l] = (0.5 * wint_ref[l].astype(F32)).T.astype(BF16)
-        bias[l] = 0.5 * column(bp_ref[l : l + 1, :])
-    bias[2] = column(cb_ref[...])
-
-    pl.semaphore_wait(barrier, len(partners))
+    bias[...] = column(cb_ref[...])
+
+    pl.semaphore_wait(barrier, expected)
     u = exchange(0, total, lambda: prepare(0))
     v = mix(0, u)
     total = layer(0, fa, fb, v, table, analysis)
@@ -337,13 +365,18 @@
     for copy in get_late:
         copy.wait()
 
-    def pooled(a, part, total):
-        return total + jnp.where((lane // 8 == a // 2) & (a >= 0), part, 0.0)
+    def pooled(parts):
+        total = jnp.zeros((64, 128), F32)
+        for a in range(GROUPS):
+            total = total + jnp.where(lane // 8 == a // 2, parts[a], 0.0)
+        return total
 
     coarse = layer(1, fb, fa, v, pool, pooled) * (1.0 / 256.0)
 
     cos, sin = devv[0:1, :], devv[1:2, :]
-    part = exact(coarse, late[:, :128])
+    high = coarse.astype(BF16).astype(F32)
+    split = jnp.where(lane < 32, high, pltpu.roll(coarse - high, 32, 1) + pltpu.roll(high, 64, 1))
+    part = dot(split.astype(BF16), sums[:128, 512:])
     part = part * cos + pltpu.roll(part, 64, 1) * sin
     acc = jnp.where(in_a32, part[:32], part[32:])
     number, slot = 16, 0
@@ -356,12 +389,12 @@
         for s in sends:
             s.start()
         if stage == 0:
-            local[...] = exact(cp_ref[...], exact(coarse, late[:, 640:])) + jnp.concatenate([bias[2]] * 4, axis=1)
+            local[...] = exact(cp_ref[...], exact(coarse, late[...])) + jnp.concatenate([bias[...]] * 4, axis=1)
             prepare(2)
         else:
             def back_step(a, carry):
                 for b in range(8):
-                    xs[pl.ds(8 * a + b, 64, stride=PAD), :] = fa[a + 1, :, b * 128 : (b + 1) * 128].astype(F32)
+                    xs[pl.ds(8 * a + b, 64, stride=PAD), :] = fa[a + 1, b].astype(F32)
                 return carry
 
             lax.fori_loop(0, GROUPS, back_step, 0)
@@ -372,7 +405,9 @@
     u = jnp.concatenate([acc, pltpu.roll(acc, 96, 1)], axis=0)
     v = mix(2, u)
     v = v * cos - pltpu.roll(v, 64, 1) * sin
-    full = exact(jnp.where(in_a, v, 0.0), late[:, 128:640]) + local[...]
+    high = v.astype(BF16)
+    split = jnp.concatenate([high, (v - high.astype(F32)).astype(BF16)], axis=1)
+    full = dot(split, sums[:, :512]) + local[...]
     for n in range(4):
         cx[n] = full[:, n * 128 : (n + 1) * 128]
 
@@ -391,7 +426,7 @@
 def local_program(consts, x, mask, w, wp, bp, win, wout, wc, cp, cb):
     hbm = pl.BlockSpec(memory_space=pltpu.HBM)
     n_remote = 16 + 38
-    names = ["table", "basis", "pool", "place", "rot", "late", "dev"]
+    names = ["table", "basis", "pool", "place", "rot", "sums", "late", "dev"]
     return pl.pallas_call(
         kernel,
         out_shape=jax.ShapeDtypeStruct((C, TX, TY), BF16),
@@ -408,30 +443,32 @@
             pltpu.VMEM((C, C), F32),
             pltpu.VMEM((1, C), F32),
             pltpu.VMEM((1024, 128), BF16),
-            pltpu.VMEM((64, 1024), BF16),
+            pltpu.VMEM((8, 64, 128), BF16),
             pltpu.VMEM((1024, 128), BF16),
             pltpu.VMEM((64, 128), BF16),
             pltpu.VMEM((48, 128), F32),
-            pltpu.VMEM((128, 1152), F32),
+            pltpu.VMEM((256, 640), BF16),
+            pltpu.VMEM((128, 512), F32),
             pltpu.VMEM((2, 128), F32),
             pltpu.VMEM((C * PAD, 128), F32),
             pltpu.VMEM((TX, TY), F32),
-            pltpu.VMEM((GROUPS + 1, C, 1024), BF16),
-            pltpu.VMEM((GROUPS + 1, C, 1024), BF16),
+            pltpu.VMEM((GROUPS + 1, 8, C, 128), BF16),
+            pltpu.VMEM((GROUPS + 1, 8, C, 128), BF16),
             pltpu.VMEM((3, 1024, 256), BF16),
             pltpu.VMEM((GROUPS, C, 128), BF16),
             pltpu.VMEM((2, C, 128), F32),
             pltpu.VMEM((2, F, C), BF16),
-            pltpu.VMEM((3, C, 128), F32),
+            pltpu.VMEM((C, 128), F32),
             pltpu.VMEM((4, C, 256), F32),
             pltpu.VMEM((4, F, 256), F32),
+            pltpu.VMEM((GROUPS + 1, C, 128), F32),
             pltpu.VMEM((2, 3, 32, 128), BF16),
             pltpu.VMEM((2, 3, 3, 32, 128), BF16),
             pltpu.VMEM((2, 32, 128), BF16),
             pltpu.VMEM((38, 32, 128), BF16),
             pltpu.VMEM((C, 512), F32),
             pltpu.VMEM((4, C, 128), F32),
-            pltpu.SemaphoreType.DMA((22,)),
+            pltpu.SemaphoreType.DMA((24,)),
             pltpu.SemaphoreType.DMA((n_remote,)),
             pltpu.SemaphoreType.DMA((n_remote,)),
         ],

time: 45.5 us -> 41.5 us (0.912)
  Pallas kernels: 44.4 us -> 40.5 us
    pallas_call x1, Pallas kernels: 44.4 us -> 40.5 us  [local_program(): pl.pallas_call(kernel, out_shape=jax.ShapeDtypeStruct((C, TX, TY), BF16),...]
where the time goes in v3:
time: 41.5 us; the launch traced here: 41.4 us
  Pallas kernels  40.5 us (98%)
  local copies, waits for them, and re-layouts  0.97 us (2%)
    pallas_call x1, Pallas kernels, local_program(): pl.pallas_call(kernel, out_shape=jax.ShapeDtypeStruct((C, TX, TY), BF16),...  40.5 us
    unnamed x1, local copies, waits for them, and re-layouts  0.97 us

profile of v3, /device:TPU:1, one launch (start us, length us, event | category | flops | bytes accessed | tf_op | source)
XLA Modules:
  0.0 41.4 jit_solution(8894625270459221880)
XLA Ops:
  0.0 40.5 %ocean.1 = bf16[64,64,128]{2,1,0:T(8,128)(2,1)S(1)} custom-call(bf16[64,64,128]{2,1,0:T(8,128)(2,1)} %x_hbm.1, s32[64,128]{1,0:T(8,128)} %mask_hbm.1, f32[2,2,2048,64]{3,2,1,0:T(8,128)} %bitcast.4, bf16[2,64,64]{2,1,0:T(8,128)(2,1)} %wp_hbm.1, f32[2,64]{1,0:T(2,128)} %bp_hbm.1, bf16[2,64,128]{2,1,0:T(8,128)(2,1)} %bitcast.6, bf16[2,64,128]{2,1,0:T(8,128)(2,1)} %wout_hbm.1, ...), custom_call_target="tpu_custom_call" | custom-call | tf_op jit(solution)/shard_map/ocean/pallas_call | solution.py:430
  40.5 1.0 %copy.20 = bf16[64,64,128]{2,1,0:T(8,128)(2,1)} copy(bf16[64,64,128]{2,1,0:T(8,128)(2,1)S(1)} %ocean.1) | data formatting | bytes 2097152

commit v4 on v3

--- a/solution.py
+++ b/solution.py
@@ -123,8 +123,7 @@
     return jnp.dot(a, b, precision=PRECISE, preferred_element_type=F32)
 
 
-XCHUNKS = 4
-UNROLL = 9
+XCHUNKS = 2
 
 
 def kernel(
@@ -166,17 +165,18 @@
         around.append((dt, dg, at(lax.rem(t + (dt + NT), NT), lax.rem(g + (dg + NG), NG))))
     yc, xc, zlo = lax.rem(t, 8), lax.div(t, 16), lax.rem(lax.div(t, 8), 2)
     zc = 2 * g + zlo
+    twin = [at(t + 1 - 2 * lax.rem(t, 2), g)]
     plane = []
     for dx in range(4):
         row = lax.rem(xc + dx, 4) * 16 + zlo * 8
-        plane += [at(row + lax.rem(yc + d, 8), g) for d in range(8) if dx or d]
+        plane += [at(row + lax.rem(yc + 2 * dy, 8), g) for dy in range(4) if dx or dy]
     along_z = []
     for d in range(1, 8):
         z = lax.rem(zc + d, 8)
         along_z.append(at(xc * 16 + lax.rem(z, 2) * 8 + yc, lax.div(z, 2)))
 
     barrier = pltpu.get_barrier_semaphore()
-    expected = jnp.int32(len(plane) + len(along_z))
+    expected = jnp.int32(len(twin) + len(plane) + len(along_z))
     for dt, dg, device in around:
         expected = expected + there(dt, dg).astype(jnp.int32)
 
@@ -184,7 +184,7 @@
         def greet(device=device):
             pl.semaphore_signal(barrier, inc=1, device_id=device, device_id_type=MESH)
 
-    for partner in along_z + plane:
+    for partner in along_z + plane + twin:
         pl.semaphore_signal(barrier, inc=1, device_id=partner, device_id_type=MESH)
 
     get_table = load(table_hbm, table)
@@ -279,19 +279,17 @@
         return jnp.concatenate([total, pltpu.roll(total, 96, 1)], axis=0)
 
     def mix(l, u):
-        sides = jnp.concatenate([u, pltpu.roll(u, 64, 1) * re_sign], axis=0).astype(BF16)
-        none = jnp.zeros_like(sides)
+        sides = jnp.concatenate([u, pltpu.roll(u, 64, 1) * re_sign], axis=0)
+        wide_a = jnp.concatenate([in_a, in_a], axis=0)
         both = jnp.concatenate(
-            [jnp.concatenate([sides, none], axis=1), jnp.concatenate([none, sides], axis=1)], axis=0
-        )
+            [jnp.where(wide_a, sides, 0.0), jnp.where(wide_a, 0.0, pltpu.roll(sides, 32, 1))], axis=0
+        ).astype(BF16)
         acc = jnp.zeros((64, 128), F32)
         for block in range(4):
             o = dot(wb[l, block * 256 : (block + 1) * 256, :], both)
             for n in range(4):
-                k = block * 4 + n
-                acc = jnp.where(mode == k, o[n * 64 : (n + 1) * 64, :128], acc)
-                acc = jnp.where(mode == k + 16, o[n * 64 : (n + 1) * 64, 128:], acc)
-        return acc
+                acc = jnp.where(mode % 16 == block * 4 + n, o[n * 64 : (n + 1) * 64], acc)
+        return jnp.where(mode < 16, acc, pltpu.roll(acc, 96, 1))
 
     def layer(l, src, dst, v, matrix, finish):
         swapped = pltpu.roll(v, 64, 1)
@@ -322,20 +320,24 @@
             sea = jnp.concatenate([jnp.concatenate(sea, axis=1)] * 4, axis=0)
             return dot(wout_ref[l], gelu_of_double(hid).astype(BF16)).astype(BF16) * sea
 
-        def step(i, carry):
-            for inner in range(UNROLL):
-                a = UNROLL * i + inner
-                for n in range(4):
-                    pre_s[n] = first(jnp.minimum(a, GROUPS - 1), n)
-                    new = third(hid_s[n], jnp.maximum(8 * a - 8 + 2 * n, 0))
-                    hid_s[(n + 2) % 4] = second(pre_s[(n + 2) % 4])
+        for a in range(GROUPS + 1):
+            for n in range(4):
+                at_step, m = 4 * a + n, (n + 2) % 4
+                if a < GROUPS:
+                    pre_s[n] = first(a, n)
+                if a > 0:
+                    new = third(hid_s[n], 8 * (a - 1) + 2 * n)
+                if 2 <= at_step < 4 * GROUPS + 2:
+                    hid_s[m] = second(pre_s[m])
+                if a > 0:
                     dst[a, 2 * n] = new[:, :128]
                     dst[a, 2 * n + 1] = new[:, 128:]
-                back = a
-                parts_s[back] = dot(jnp.concatenate([dst[back, b] for b in range(8)], axis=1), matrix[...])
-            return carry
-
-        lax.fori_loop(0, (GROUPS + 1) // UNROLL, step, 0)
+                if a > 1 and n < 2:
+                    half = slice(512 * n, 512 * n + 512)
+                    piece = dot(jnp.concatenate([dst[a - 1, b] for b in range(4 * n, 4 * n + 4)], axis=1), matrix[half, :])
+                    parts_s[a - 1] = piece if n == 0 else parts_s[a - 1] + piece
+        parts_s[GROUPS] = dot(jnp.concatenate([dst[GROUPS, b] for b in range(8)], axis=1), matrix[...])
+
         return finish([parts_s[a + 1] for a in range(GROUPS)])
 
     def analysis(parts):
@@ -379,27 +381,28 @@
     part = dot(split.astype(BF16), sums[:128, 512:])
     part = part * cos + pltpu.roll(part, 64, 1) * sin
     acc = jnp.where(in_a32, part[:32], part[32:])
-    number, slot = 16, 0
-    for stage, peers in enumerate((plane, along_z)):
+    slot = 0
+    for stage, peers in enumerate((twin, plane, along_z)):
         csend[stage] = acc.astype(BF16)
         sends = []
         for peer in peers:
-            sends.append(remote(csend.at[stage], crecv.at[slot], number, peer))
-            number, slot = number + 1, slot + 1
+            sends.append(remote(csend.at[stage], crecv.at[slot], 16 + stage, peer))
+            slot += 1
         for s in sends:
             s.start()
-        if stage == 0:
+        if stage == 1:
             local[...] = exact(cp_ref[...], exact(coarse, late[...])) + jnp.concatenate([bias[...]] * 4, axis=1)
             prepare(2)
-        else:
+        if stage == 2:
             def back_step(a, carry):
                 for b in range(8):
                     xs[pl.ds(8 * a + b, 64, stride=PAD), :] = fa[a + 1, b].astype(F32)
                 return carry
 
             lax.fori_loop(0, GROUPS, back_step, 0)
-        for s in sends:
-            s.wait()
+        landed = crecv.at[pl.ds(slot - len(peers), len(peers))]
+        for sem in (ssem, rsem):
+            pltpu.make_async_copy(landed, landed, sem.at[16 + stage]).wait()
         for n in range(slot - len(peers), slot):
             acc = acc + crecv[n].astype(F32)
     u = jnp.concatenate([acc, pltpu.roll(acc, 96, 1)], axis=0)
@@ -425,7 +428,7 @@
 
 def local_program(consts, x, mask, w, wp, bp, win, wout, wc, cp, cb):
     hbm = pl.BlockSpec(memory_space=pltpu.HBM)
-    n_remote = 16 + 38
+    n_remote = 16 + 3
     names = ["table", "basis", "pool", "place", "rot", "sums", "late", "dev"]
     return pl.pallas_call(
         kernel,
@@ -464,11 +467,11 @@
             pltpu.VMEM((GROUPS + 1, C, 128), F32),
             pltpu.VMEM((2, 3, 32, 128), BF16),
             pltpu.VMEM((2, 3, 3, 32, 128), BF16),
-            pltpu.VMEM((2, 32, 128), BF16),
-            pltpu.VMEM((38, 32, 128), BF16),
+            pltpu.VMEM((3, 32, 128), BF16),
+            pltpu.VMEM((23, 32, 128), BF16),
             pltpu.VMEM((C, 512), F32),
             pltpu.VMEM((4, C, 128), F32),
-            pltpu.SemaphoreType.DMA((24,)),
+            pltpu.SemaphoreType.DMA((21,)),
             pltpu.SemaphoreType.DMA((n_remote,)),
             pltpu.SemaphoreType.DMA((n_remote,)),
         ],

time: 41.5 us -> 40.1 us (0.966)
  Pallas kernels: 40.5 us -> 38.9 us
    pallas_call x1, Pallas kernels: 40.5 us -> 38.9 us  [local_program(): pl.pallas_call(kernel, out_shape=jax.ShapeDtypeStruct((C, TX, TY), BF16),...]
where the time goes in v4:
time: 40.1 us; the launch traced here: 39.9 us
  Pallas kernels  38.9 us (97%)
  local copies, waits for them, and re-layouts  0.97 us (2%)
    pallas_call x1, Pallas kernels, local_program(): pl.pallas_call(kernel, out_shape=jax.ShapeDtypeStruct((C, TX, TY), BF16),...  38.9 us
    unnamed x1, local copies, waits for them, and re-layouts  0.97 us

profile of v4, /device:TPU:1, one launch (start us, length us, event | category | flops | bytes accessed | tf_op | source)
XLA Modules:
  0.0 39.9 jit_solution(17893415231269811488)
XLA Ops:
  0.0 38.9 %ocean.1 = bf16[64,64,128]{2,1,0:T(8,128)(2,1)S(1)} custom-call(bf16[64,64,128]{2,1,0:T(8,128)(2,1)} %x_hbm.1, s32[64,128]{1,0:T(8,128)} %mask_hbm.1, f32[2,2,2048,64]{3,2,1,0:T(8,128)} %bitcast.4, bf16[2,64,64]{2,1,0:T(8,128)(2,1)} %wp_hbm.1, f32[2,64]{1,0:T(2,128)} %bp_hbm.1, bf16[2,64,128]{2,1,0:T(8,128)(2,1)} %bitcast.6, bf16[2,64,128]{2,1,0:T(8,128)(2,1)} %wout_hbm.1, ...), custom_call_target="tpu_custom_call" | custom-call | tf_op jit(solution)/shard_map/ocean/pallas_call | solution.py:433
  38.9 1.0 %copy.20 = bf16[64,64,128]{2,1,0:T(8,128)(2,1)} copy(bf16[64,64,128]{2,1,0:T(8,128)(2,1)S(1)} %ocean.1) | data formatting | bytes 2097152
